TPU v7x, 256 devices: a whole 4x4x8 slice. The times are simulated.
256 devices in a mesh: dp: 32 (over x, z), frame: 8 (over y, core).
Axes of the slice: x: 4, y: 4, z: 8, core: 2. Of those that a mesh axis runs over, the one named last changes fastest.
Arguments:
- features: bfloat16 [32, 16, 32, 64, 128], P('dp', 'frame'), may hold values from -6 to 6
- vis_block: int32 [32, 16, 16, 2], P('dp', None, 'frame'), may hold values from 0 to 31
- vis_count: int32 [32, 16, 16], P('dp', None, 'frame'), may hold values from 1 to 2
- query_frame: int32 [32, 256], P('dp'), may hold values from 0 to 15
- query_block: int32 [32, 256], P('dp'), may hold values from 0 to 31
- query_cell: int32 [32, 256], P('dp'), may hold values from 0 to 63
- cotangent: bfloat16 [32, 4, 256, 16], P('dp', None, 'frame')
- w_in: bfloat16 [128, 384], replicated, may hold values from -0.5 to 0.5
- gain: float32 [384], replicated, may hold values from 0.1 to 1.9
- w_qkv: bfloat16 [384, 1152], replicated, may hold values from -0.3125 to 0.3125
- w_out: bfloat16 [384, 384], replicated, may hold values from -0.3125 to 0.3125
- w_head: bfloat16 [4, 384], replicated, may hold values from -0.3125 to 0.3125
Outputs:
- grad_in: float32 [128, 384], replicated
- grad_gain: float32 [384], replicated
- grad_qkv: float32 [384, 1152], replicated
- grad_out: float32 [384, 384], replicated
- grad_head: float32 [4, 384], replicated
Inputs may be any that keep to these rules, and one draw needn't show every extreme that they name: vis_count counts the leading visible slots of vis_block.
All inputs are finite; a program needn't handle non-finite values.
Results may differ from a plain program's by a relative error of at most 0.012.
Values may be sent and summed in bfloat16 or wider, within the bound.
No kernel may reach another device: no remote copies, remote signals or barrier semaphores. Data moves between devices by JAX's collectives and lax.ppermute only.
A program may use at most 64 MiB of HBM per device.

v0:
```python
import jax
import jax.numpy as jnp
from jax import lax
from jax.sharding import PartitionSpec as P

HEADS = 8


def attend(query, keys, values):
    scale = query.shape[-1] ** (-0.5)
    scores = (
        jnp.einsum("nfhd,nghd->nhfg", query.astype(jnp.float32), keys.astype(jnp.float32)) * scale
    )
    probs = jax.nn.softmax(scores, axis=-1).astype(jnp.bfloat16)
    probs = lax.optimization_barrier(probs)
    mixed = jnp.einsum("nhfg,nghd->nfhd", probs.astype(jnp.float32), values.astype(jnp.float32))
    return mixed.astype(jnp.bfloat16)


def inner_rows(left, right):
    return lax.dot_general(
        left, right, (((0,), (0,)), ((), ())), preferred_element_type=jnp.float32
    )


def outer_cols(left, right):
    return lax.dot_general(
        left, right, (((1,), (1,)), ((), ())), preferred_element_type=jnp.float32
    )


def local_grads(corr, cot, w_in, gain, w_qkv, w_out, w_head):
    tracks, frames, width = corr.shape
    total = tracks * frames
    hid = w_in.shape[1]
    head_size = hid // HEADS
    rows = corr.reshape(total, width)
    x_zero = jnp.dot(rows, w_in, preferred_element_type=jnp.float32)
    centred = x_zero - jnp.mean(x_zero, axis=-1, keepdims=True)
    inv_std = lax.rsqrt(jnp.mean(centred * centred, axis=-1, keepdims=True) + 1e-05)
    normed = centred * inv_std
    hidden = (normed * gain).astype(jnp.bfloat16)
    qkv = jnp.dot(hidden, w_qkv, preferred_element_type=jnp.float32).astype(jnp.bfloat16)
    split = qkv.reshape(tracks, frames, 3, HEADS, head_size)
    mixed, backward = jax.vjp(attend, split[:, :, 0], split[:, :, 1], split[:, :, 2])
    mixed = mixed.reshape(total, hid)
    y_out = (x_zero + jnp.dot(mixed, w_out, preferred_element_type=jnp.float32)).astype(
        jnp.bfloat16
    )
    ct_rows = cot.reshape(cot.shape[0], total)
    g_head = jnp.dot(ct_rows, y_out, preferred_element_type=jnp.float32)
    d_y = inner_rows(ct_rows, w_head)
    d_y16 = d_y.astype(jnp.bfloat16)
    g_out = inner_rows(mixed, d_y16)
    d_mixed = outer_cols(d_y16, w_out).astype(jnp.bfloat16)
    d_q, d_k, d_v = backward(d_mixed.reshape(tracks, frames, HEADS, head_size))
    d_qkv = jnp.stack([d_q, d_k, d_v], axis=2).reshape(total, 3 * hid)
    g_qkv = inner_rows(hidden, d_qkv)
    d_hidden = outer_cols(d_qkv, w_qkv)
    g_gain = jnp.sum(d_hidden * normed, axis=0)
    d_norm = d_hidden * gain
    d_x = (
        inv_std
        * (
            d_norm
            - jnp.mean(d_norm, axis=-1, keepdims=True)
            - normed * jnp.mean(d_norm * normed, axis=-1, keepdims=True)
        )
        + d_y
    )
    d_x16 = d_x.astype(jnp.bfloat16)
    g_in = inner_rows(rows, d_x16)
    return (g_in, g_gain, g_qkv, g_out, g_head)


def body(
    features,
    vis_block,
    vis_count,
    query_frame,
    query_block,
    query_cell,
    cotangent,
    w_in,
    gain,
    w_qkv,
    w_out,
    w_head,
):
    feats = features[0]
    fr_dev = feats.shape[0]
    cells = feats.shape[2]
    width = feats.shape[3]
    trk_dev = cotangent.shape[2]
    frame_pos = lax.axis_index("frame")
    frames_q = query_frame[0]
    blocks_q = query_block[0]
    cells_q = query_cell[0]
    local = frames_q - frame_pos * fr_dev
    inside = (local >= 0) & (local < fr_dev)
    picked = feats[jnp.clip(local, 0, fr_dev - 1), blocks_q, cells_q].astype(jnp.float32)
    query = lax.psum_scatter(
        jnp.where(inside[:, None], picked, 0.0).astype(jnp.bfloat16),
        "frame",
        scatter_dimension=0,
        tiled=True,
    )
    groups = vis_block.shape[1]
    slots = vis_block.shape[3]
    frame_ids = jnp.arange(fr_dev, dtype=jnp.int32)[None, :, None]
    patches = feats[frame_ids, vis_block[0]]
    live = jnp.arange(slots, dtype=jnp.int32)[None, None, :] < vis_count[0][:, :, None]
    patches = jnp.where(live[..., None, None], patches, jnp.zeros((), jnp.bfloat16))
    scale = width ** (-0.5)
    outgoing = patches.reshape(groups, fr_dev, slots, cells * width)
    arrived = lax.all_to_all(outgoing, "frame", split_axis=0, concat_axis=1, tiled=True)
    own_groups = arrived.shape[0]
    all_frames = arrived.shape[1]
    arrived = arrived.reshape(own_groups, all_frames, slots, cells, width)
    corr = jnp.einsum(
        "gtc,gfkpc->gtfkp",
        query.reshape(own_groups, -1, width),
        arrived,
        preferred_element_type=jnp.float32,
    )
    corr = (corr * scale).astype(jnp.bfloat16).reshape(trk_dev, all_frames, slots * cells)
    g_in, g_gain, g_qkv, g_out, g_head = local_grads(
        corr, cotangent[0], w_in, gain, w_qkv, w_out, w_head
    )
    s_in, s_gain, s_qkv, s_out, s_head = lax.psum(
        (g_in, g_gain, g_qkv, g_out, g_head), ("dp", "frame")
    )
    return (s_in, s_gain, s_qkv, s_out, s_head)


def solution(mesh):
    in_specs = (
        P("dp", "frame", None, None, None),
        P("dp", None, "frame", None),
        P("dp", None, "frame"),
        P("dp", None),
        P("dp", None),
        P("dp", None),
        P("dp", None, "frame", None),
        P(),
        P(),
        P(),
        P(),
        P(),
    )
    out_specs = (P(), P(), P(), P(), P())
    return jax.shard_map(body, mesh=mesh, in_specs=in_specs, out_specs=out_specs, check_vma=False)
```

profile of v0, /device:TPU:1, one launch (start us, length us, event | category | flops | bytes accessed | tf_op | source)
XLA Modules:
  0.0 382.8 jit_solution(13826835870761128297)
XLA Ops:
  7.2 0.8 fusion.27
  8.1 0.1 reshape.207
  8.2 0.2 copy-done
  8.4 0.8 gather_fusion.1
  9.2 0.3 gather.10
  9.7 1.9 broadcast_select_fusion
  11.7 7.3 %all-to-all-start = ((bf16[16,2,2,8192]{3,2,1,0:T(2,128)(2,1)}), bf16[16,2,2,8192]{3,2,1,0:T(2,128)(2,1)}, u32[]{:S(2)}, u32[]{:S(2)}) async-start(bf16[16,2,2,8192]{3,2,1,0:T(2,128)(2,1)} %broadcast_select_fusion), calls=%async_computation.1 | async-start | bytes 2097152 | tf_op jit(solution)/shard_map/all_to_all | solution.py:116
  19.0 1.9 gather_fusion
  21.0 0.7 select_convert_fusion
  22.0 0.3 fusion.43
  22.3 1.2 copy.40
  23.5 0.4 convolution_convert_fusion.6
  23.9 1.9 reshape.197
  25.8 8.3 %all-to-all-done = bf16[16,2,2,8192]{3,2,1,0:T(2,128)(2,1)} async-done(((bf16[16,2,2,8192]{3,2,1,0:T(2,128)(2,1)}), bf16[16,2,2,8192]{3,2,1,0:T(2,128)(2,1)}, u32[]{:S(2)}, u32[]{:S(2)}) %all-to-all-start) | async-done | bytes 1048608 | tf_op jit(solution)/shard_map/all_to_all | solution.py:116
  34.1 3.4 copy.29
  37.5 2.7 reshape.196
  40.2 15.1 %reduce-scatter.2.cloned.1.call-done = bf16[32,128]{1,0:T(8,128)(2,1)} async-done(((bf16[256,128]{1,0:T(8,128)(2,1)}), bf16[32,128]{1,0:T(8,128)(2,1)}) %reduce-scatter.2.cloned.1.call-update) | async-done | bytes 8208 | tf_op jit(solution)/shard_map/reduce_scatter | solution.py:102
  55.3 2.1 fusion.13
  57.4 0.2 copy.30
  57.6 0.1 reshape_reshape.3
  57.8 0.3 fusion.41
  58.1 0.1 multiply_reduce_fusion.3
  58.3 3.1 convolution_convert_fusion
  61.4 5.3 %reshape.198 = bf16[32,16,3,8,48]{4,3,2,1,0:T(8,128)(2,1)} reshape(bf16[512,1152]{1,0:T(8,128)(2,1)} %convolution_convert_fusion) | data formatting | bytes 2359296 | tf_op jit(solution)/shard_map/reshape | solution.py:44
  66.7 3.7 fusion.40
  70.4 3.8 fusion.42
  74.2 2.3 convolution_convert_fusion.5
  76.6 1.9 fusion.5
  78.5 1.9 fusion.7
  80.4 2.5 fusion.8
  83.0 1.6 fusion.10
  84.6 0.5 fusion.9
  85.1 0.8 pad_maximum_fusion
  85.9 2.5 copy.39
  88.4 5.0 %reshape.199 = bf16[512,1152]{1,0:T(8,128)(2,1)} reshape(bf16[32,16,3,8,48]{4,3,2,1,0:T(8,128)(2,1)} %copy.39) | data formatting | bytes 2359296 | tf_op jit(solution)/shard_map/reshape | solution.py:57
  93.4 3.3 multiply_reduce_fusion.1
  96.7 1.9 fusion.37
  98.6 1.2 copy.41
  99.9 2.0 reshape.200
  101.9 1.2 fusion.22
  103.2 0.2 copy-done.10
  103.4 1.1 fusion.21
  104.5 0.5 fusion.14
  105.1 78.3 %all-reduce = (f32[384]{0:T(512)}, f32[4,384]{1,0:T(4,128)}) all-reduce(f32[384]{0:T(512)S(1)} %get-tuple-element.5, f32[4,384]{1,0:T(4,128)S(1)} %fusion.14), channel_id=1, replica_groups=mesh['dp'=32,'frame'=8] {'dp','frame'}, use_global_device_ids=true, to_apply=%region_10.11 | all-reduce | flops 1920 | bytes 15360 | tf_op jit(solution)/shard_map/psum | solution.py:130
  183.3 187.3 %all-reduce.4.cloned.1.call-done = (f32[128,384]{1,0:T(8,128)}, f32[384,1152]{1,0:T(8,128)}, f32[384,384]{1,0:T(8,128)}) async-done(((f32[128,384]{1,0:T(8,128)}, f32[384,1152]{1,0:T(8,128)}, f32[384,384]{1,0:T(8,128)}), (f32[128,384]{1,0:T(8,128)}, f32[384,1152]{1,0:T(8,128)}, f32[384,384]{1,0:T(8,128)})) %all-reduce.4.cloned.1.call-update) | async-done | bytes 2555920 | tf_op jit(solution)/shard_map/psum | solution.py:130
  370.6 1.7 copy.85
  372.3 2.8 copy.86
  375.1 0.8 copy.87
  (54 shorter events, 0.7 us)
Async XLA Ops:
  7.2 1.2 copy-start
  8.4 1.1 copy-start.17
  9.7 9.3 %copy-start.15 = (s32[1,256]{1,0:T(1,128)S(1)}, s32[1,256]{1,0:T(1,128)}, u32[]{:S(2)}) copy-start(s32[1,256]{1,0:T(1,128)} %param.15) | copy-start | bytes 3076
  9.7 9.3 %copy-start.18 = (s32[1,256]{1,0:T(1,128)S(1)}, s32[1,256]{1,0:T(1,128)}, u32[]{:S(2)}) copy-start(s32[1,256]{1,0:T(1,128)} %param.17) | copy-start | bytes 3076
  9.7 9.3 %copy-start.19 = (s32[1,256]{1,0:T(1,128)S(1)}, s32[1,256]{1,0:T(1,128)}, u32[]{:S(2)}) copy-start(s32[1,256]{1,0:T(1,128)} %param.16) | copy-start | bytes 3076
  9.7 12.1 %copy-start.14 = (bf16[1,4,32,16]{2,3,1,0:T(8,128)(2,1)S(1)}, bf16[1,4,32,16]{2,3,1,0:T(8,128)(2,1)}, u32[]{:S(2)}) copy-start(bf16[1,4,32,16]{2,3,1,0:T(8,128)(2,1)} %param.18) | copy-start | bytes 12292
  9.7 12.3 %copy-start.16 = (bf16[4,384]{1,0:T(4,128)(2,1)S(1)}, bf16[4,384]{1,0:T(4,128)(2,1)}, u32[]{:S(2)}) copy-start(bf16[4,384]{1,0:T(4,128)(2,1)} %param.23) | copy-start | bytes 9220
  11.7 22.4 %all-to-all-start = ((bf16[16,2,2,8192]{3,2,1,0:T(2,128)(2,1)}), bf16[16,2,2,8192]{3,2,1,0:T(2,128)(2,1)}, u32[]{:S(2)}, u32[]{:S(2)}) async-start(bf16[16,2,2,8192]{3,2,1,0:T(2,128)(2,1)} %broadcast_select_fusion), calls=%async_computation.1 | async-start | bytes 2097152 | tf_op jit(solution)/shard_map/all_to_all | solution.py:116
  19.0 4.5 %copy-start.7 = (bf16[384,384]{1,0:T(8,128)(2,1)S(1)}, bf16[384,384]{1,0:T(8,128)(2,1)}, u32[]{:S(2)}) copy-start(bf16[384,384]{1,0:T(8,128)(2,1)} %param.22) | copy-start | bytes 884740
  19.0 36.3 %reduce-scatter.2.cloned.1.call-start = ((), (), s32[]{:S(2)}) async-start(), calls=%async_computation.2 | async-start | bytes 73728 | tf_op jit(solution)/shard_map/reduce_scatter | solution.py:102
  21.7 348.9 %all-reduce.4.cloned.1.call-start = ((), (), s32[]{:S(2)}) async-start(), calls=%async_computation.3 | async-start | bytes 5111808 | tf_op jit(solution)/shard_map/psum | solution.py:130
  37.5 20.3 %copy-start.12 = (bf16[128,384]{1,0:T(8,128)(2,1)S(1)}, bf16[128,384]{1,0:T(8,128)(2,1)}, u32[]{:S(2)}) copy-start(bf16[128,384]{1,0:T(8,128)(2,1)} %param.19) | copy-start | bytes 294916
  40.2 18.1 %copy-start.13 = (f32[384]{0:T(512)S(1)}, f32[384]{0:T(512)}, u32[]{:S(2)}) copy-start(f32[384]{0:T(512)} %param.20) | copy-start | bytes 4612
  74.2 2.4 copy-start.6
  76.6 1.9 copy-start.9
  78.5 1.9 copy-start.8
  80.4 2.5 copy-start.2
  82.9 1.7 copy-start.1
  93.4 3.3 copy-start.3
  96.7 1.9 copy-start.4
  101.9 1.2 copy-start.5
  101.9 1.5 copy-start.10
  370.6 4.5 %copy-start.11 = (f32[384,384]{1,0:T(8,128)S(1)}, f32[384,384]{1,0:T(8,128)}, u32[]{:S(2)}) copy-start(f32[384,384]{1,0:T(8,128)} %get-tuple-element.28) | copy-start | bytes 1769476
Sparse Core Ops, SparseCore 0:
  22.8 32.3 reduce-scatter.1
  104.6 265.9 all-reduce.3
where the time goes:
time: 384 us; the launch traced here: 383 us
  waiting for transfers between devices  211 us (55%)
  blocking collectives  78.3 us (20%)
  local copies, waits for them, and re-layouts  38.5 us (10%)
  matrix products  27.1 us (7%)
  between operations  14.4 us (4%)
  starting transfers between devices  7.35 us (2%)
  other arithmetic  6.41 us (2%)
    psum x1, waiting for transfers between devices, body(): lax.psum((g_in, g_gain, g_qkv, g_out, g_head), ('dp', 'frame'))  187 us
    psum x1, blocking collectives, body(): lax.psum((g_in, g_gain, g_qkv, g_out, g_head), ('dp', 'frame'))  78.3 us
    reduce_scatter x1, waiting for transfers between devices, body(): lax.psum_scatter(jnp.where(inside[:, None], picked, 0.0).astype(jnp.bfloa...  15.1 us
    all_to_all x1, waiting for transfers between devices, body(): lax.all_to_all(outgoing, 'frame', split_axis=0, concat_axis=1, tiled=True)  8.32 us
  transfers between devices with their start and end apart: 3, of which 3 were waited for; matrix products, arithmetic and copies ran while one was open for 3% of the time, Pallas kernels for 0%

commit v1 on v0

v1 whole, which is shorter than its diff:
```python
import jax
import jax.numpy as jnp
from jax import lax
from jax.experimental import pallas as pl
from jax.experimental.pallas import tpu as pltpu
from jax.sharding import PartitionSpec as P

HEADS = 8
SIZE = 48
HID = 384
TOK = 512
ROWS = 5120
F32 = jnp.float32
BF16 = jnp.bfloat16


def dot(left, right, dims=((1,), (0,))):
    return lax.dot_general(left, right, (dims, ((), ())), preferred_element_type=F32)


NT = ((1,), (1,))
TN = ((0,), (0,))


def token_kernel(
    pat_ref,
    qry_ref,
    ct_ref,
    w_in_t,
    gain_ref,
    w_qkv_t,
    w_qkv,
    w_out_t,
    w_out,
    w_head,
    out_ref,
    corr32,
    corr16,
    x_zero,
    normed,
    hidden,
    qkv,
    mixed,
    d_y,
    d_y16,
    d_mixed,
    d_qkv,
    inv_ref,
):
    query = jnp.sum(qry_ref[...].astype(F32), axis=0).astype(BF16)
    scale = 128 ** (-0.5)
    for g in range(2):
        for s in range(8):
            part = dot(query[g * 16 : g * 16 + 16], pat_ref[s, g * 256 : g * 256 + 256], NT) * scale
            for half in range(2):
                for fr in range(2):
                    row = (g * 2 + half) * 128 + (s * 2 + fr) * 8
                    corr32[row : row + 8, :] = part[half * 8 : half * 8 + 8, fr * 128 : fr * 128 + 128]
    corr16[...] = corr32[...].astype(BF16)

    ct = ct_ref[...]
    for c in range(2):
        cols = slice(c * 256, c * 256 + 256)
        x0 = dot(w_in_t[...], corr16[cols, :], NT)
        x_zero[:, cols] = x0
        mean = jnp.mean(x0, axis=0, keepdims=True)
        centred = x0 - mean
        inv = lax.rsqrt(jnp.mean(centred * centred, axis=0, keepdims=True) + 1e-05)
        nrm = centred * inv
        inv_ref[:, cols] = jnp.broadcast_to(inv, (8, 256))
        normed[:, cols] = nrm
        hid = (nrm * gain_ref[:, :1]).astype(BF16)
        hidden[:, cols] = hid
        for r in range(3):
            rows = slice(r * 384, r * 384 + 384)
            qkv[rows, cols] = dot(w_qkv_t[rows, :], hid).astype(BF16)
        dy = dot(w_head[...], ct[:, cols], TN)
        d_y[:, cols] = dy
        dy16 = dy.astype(BF16)
        d_y16[:, cols] = dy16
        d_mixed[:, cols] = dot(w_out[...], dy16).astype(BF16)

    own = (
        lax.broadcasted_iota(jnp.int32, (8, 128), 0)
        == lax.broadcasted_iota(jnp.int32, (8, 128), 1) % 8
    ).astype(F32)
    a_scale = SIZE ** (-0.5)

    def block(b, carry):
        cols = pl.ds(pl.multiple_of(b * 128, 128), 128)
        for h in range(HEADS):
            rq = slice(h * SIZE, h * SIZE + SIZE)
            rk = slice(HID + h * SIZE, HID + h * SIZE + SIZE)
            rv = slice(2 * HID + h * SIZE, 2 * HID + h * SIZE + SIZE)
            q_t, k_t, v_t = qkv[rq, cols], qkv[rk, cols], qkv[rv, cols]
            d_a = d_mixed[rq, cols]
            score = dot(k_t, q_t, TN).reshape(16, 8, 128) * a_scale
            expo = jnp.exp(score - jnp.max(score, axis=0, keepdims=True))
            prob = expo * (own / jnp.sum(expo, axis=0))[None]
            prob16 = prob.reshape(128, 128).astype(BF16)
            mixed[rq, cols] = dot(v_t, prob16).astype(BF16)
            d_p = dot(v_t, d_a, TN).astype(BF16).astype(F32).reshape(16, 8, 128)
            inner = jnp.sum(d_p * prob, axis=0, keepdims=True)
            d_s = (prob * (d_p - inner) * a_scale).reshape(128, 128).astype(BF16)
            d_qkv[rq, cols] = dot(k_t, d_s).astype(BF16)
            d_qkv[rk, cols] = dot(q_t, d_s, NT).astype(BF16)
            d_qkv[rv, cols] = dot(d_a, prob16, NT).astype(BF16)
        return carry

    lax.fori_loop(0, 4, block, 0)

    head = jnp.zeros((16, HID), F32)
    gain_sum = jnp.zeros((HID, 128), F32)
    g_in = jnp.zeros((128, HID), F32)
    for c in range(2):
        cols = slice(c * 256, c * 256 + 256)
        y16 = (x_zero[:, cols] + dot(w_out_t[...], mixed[:, cols])).astype(BF16)
        head = head + dot(ct[:, cols], y16, NT)
        dh = dot(w_qkv[...], d_qkv[:, cols])
        nrm = normed[:, cols]
        prod = dh * nrm
        gain_sum = gain_sum + prod[:, :128] + prod[:, 128:]
        gain = gain_ref[:, :1]
        dn = dh * gain
        m_one = jnp.mean(dn, axis=0, keepdims=True)
        m_two = jnp.mean(dn * nrm, axis=0, keepdims=True)
        dx = inv_ref[:1, cols] * (dn - m_one - nrm * m_two) + d_y[:, cols]
        g_in = g_in + dot(corr16[cols, :], dx.astype(BF16), ((0,), (1,)))
    for j in range(9):
        part = dot(hidden[...], d_qkv[j * 128 : j * 128 + 128, :], NT)
        out_ref[j * 384 : j * 384 + 384, :] = part.astype(BF16)
    for j in range(3):
        part = dot(mixed[...], d_y16[j * 128 : j * 128 + 128, :], NT)
        out_ref[3456 + j * 384 : 3456 + j * 384 + 384, :] = part.astype(BF16)
    gain_row = jnp.sum(gain_sum.T, axis=0, keepdims=True)
    at_four = lax.broadcasted_iota(jnp.int32, (16, HID), 0) == 4
    head = jnp.where(at_four, jnp.broadcast_to(gain_row, (16, HID)), head)
    for j in range(3):
        lanes = slice(j * 128, j * 128 + 128)
        out_ref[4608 + j * 128 : 4736 + j * 128, :] = g_in[:, lanes].astype(BF16)
        out_ref[4992 + j * 16 : 5008 + j * 16, :] = head[:, lanes].astype(BF16)
    out_ref[5040:ROWS, :] = jnp.zeros((ROWS - 5040, 128), BF16)


def token_grads(pat, qry, ct, w_in_t, gain, w_qkv_t, w_qkv, w_out_t, w_out, w_head):
    vm = pl.BlockSpec(memory_space=pltpu.VMEM)
    return pl.pallas_call(
        token_kernel,
        out_shape=jax.ShapeDtypeStruct((ROWS, 128), BF16),
        in_specs=[vm] * 10,
        out_specs=vm,
        scratch_shapes=[
            pltpu.VMEM((TOK, 128), F32),
            pltpu.VMEM((TOK, 128), BF16),
            pltpu.VMEM((HID, TOK), F32),
            pltpu.VMEM((HID, TOK), F32),
            pltpu.VMEM((HID, TOK), BF16),
            pltpu.VMEM((3 * HID, TOK), BF16),
            pltpu.VMEM((HID, TOK), BF16),
            pltpu.VMEM((HID, TOK), F32),
            pltpu.VMEM((HID, TOK), BF16),
            pltpu.VMEM((HID, TOK), BF16),
            pltpu.VMEM((3 * HID, TOK), BF16),
            pltpu.VMEM((8, TOK), F32),
        ],
        name="token_grads",
    )(pat, qry, ct, w_in_t, gain, w_qkv_t, w_qkv, w_out_t, w_out, w_head)


def unpack_kernel(x_ref, g_in, g_gain, g_qkv, g_out, g_head):
    for j in range(9):
        g_qkv[:, j * 128 : j * 128 + 128] = x_ref[j * 384 : j * 384 + 384, :].astype(F32)
    for j in range(3):
        lanes = slice(j * 128, j * 128 + 128)
        g_out[:, lanes] = x_ref[3456 + j * 384 : 3840 + j * 384, :].astype(F32)
        g_in[:, lanes] = x_ref[4608 + j * 128 : 4736 + j * 128, :].astype(F32)
        tail = x_ref[4992 + j * 16 : 5008 + j * 16, :].astype(F32)
        g_head[:, lanes] = tail[:4]
        g_gain[:, lanes] = tail[4:5]


def unpack(x):
    vm = pl.BlockSpec(memory_space=pltpu.VMEM)
    g_in, g_gain, g_qkv, g_out, g_head = pl.pallas_call(
        unpack_kernel,
        out_shape=(
            jax.ShapeDtypeStruct((128, HID), F32),
            jax.ShapeDtypeStruct((1, HID), F32),
            jax.ShapeDtypeStruct((HID, 3 * HID), F32),
            jax.ShapeDtypeStruct((HID, HID), F32),
            jax.ShapeDtypeStruct((4, HID), F32),
        ),
        in_specs=[vm],
        out_specs=(vm,) * 5,
        name="unpack",
    )(x)
    return g_in, g_gain.reshape(HID), g_qkv, g_out, g_head


def swap(x, axis):
    return lax.all_to_all(x, axis, split_axis=0, concat_axis=0, tiled=True)


def fold(x, n):
    return jnp.sum(x.reshape(n, x.shape[0] // n, x.shape[1]).astype(F32), axis=0).astype(BF16)


def sum_all(x):
    x = fold(swap(x, "frame"), 8)
    x = fold(swap(x, "dp"), 32)
    x = swap(jnp.tile(x, (32, 1)), "dp")
    return swap(jnp.tile(x, (8, 1)), "frame")


def body(
    features,
    vis_block,
    vis_count,
    query_frame,
    query_block,
    query_cell,
    cotangent,
    w_in,
    gain,
    w_qkv,
    w_out,
    w_head,
):
    feats = features[0]
    fr_dev = feats.shape[0]
    frame_pos = lax.axis_index("frame")
    local = query_frame[0] - frame_pos * fr_dev
    inside = (local >= 0) & (local < fr_dev)
    picked = feats[jnp.clip(local, 0, fr_dev - 1), query_block[0], query_cell[0]]
    picked = jnp.where(inside[:, None], picked, jnp.zeros((), BF16))
    queries = swap(picked, "frame").reshape(8, 32, 128)
    frame_ids = jnp.arange(fr_dev, dtype=jnp.int32)[None, :, None]
    patches = feats[frame_ids, vis_block[0]]
    live = jnp.arange(2, dtype=jnp.int32)[None, None, :] < vis_count[0][:, :, None]
    patches = jnp.where(live[..., None, None], patches, jnp.zeros((), BF16))
    arrived = swap(patches.reshape(16 * 256, 128), "frame").reshape(8, 512, 128)
    ct = cotangent[0].reshape(4, 4, 8, 16).transpose(0, 1, 3, 2).reshape(4, TOK)
    ct = jnp.pad(ct, ((0, 12), (0, 0)))
    packed = token_grads(
        arrived,
        queries,
        ct,
        w_in.T,
        jnp.broadcast_to(gain[:, None], (HID, 128)),
        w_qkv.T,
        w_qkv,
        w_out.T,
        w_out,
        jnp.pad(w_head, ((0, 12), (0, 0))),
    )
    return unpack(sum_all(packed))


def solution(mesh):
    in_specs = (
        P("dp", "frame", None, None, None),
        P("dp", None, "frame", None),
        P("dp", None, "frame"),
        P("dp", None),
        P("dp", None),
        P("dp", None),
        P("dp", None, "frame", None),
        P(),
        P(),
        P(),
        P(),
        P(),
    )
    out_specs = (P(), P(), P(), P(), P())
    return jax.shard_map(body, mesh=mesh, in_specs=in_specs, out_specs=out_specs, check_vma=False)
```

time: 384 us -> 139 us (0.36)
  waiting for transfers between devices: 211 us -> 11 us
  local copies, waits for them, and re-layouts: 38.5 us -> 9.84 us
  matrix products: 27.1 us -> 0 us
  Pallas kernels: 0 us -> 19.6 us
  between operations: 14.4 us -> 0.75 us
    psum x1 -> x0, waiting for transfers between devices: 187 us -> none  [body(): lax.psum((g_in, g_gain, g_qkv, g_out, g_head), ('dp', 'frame'))]
    all_to_all x0 -> x4, blocking collectives: none -> 80.2 us  [swap(): return lax.all_to_all(x, axis, split_axis=0, concat_axis=0, tiled=True)]
    psum x1 -> x0, blocking collectives: 78.3 us -> none  [body(): lax.psum((g_in, g_gain, g_qkv, g_out, g_head), ('dp', 'frame'))]
    dot_general x15 -> x0, matrix products: 23.3 us -> none  [the longest x4 4.57 us: inner_rows(): lax.dot_general(left, right, (((0,), (0,)), ((), ())), preferred_element_...]
    pallas_call x0 -> x2, Pallas kernels: none -> 19.6 us  [the longest x1 16.8 us: token_grads(): pl.pallas_call(token_kernel, out_shape=jax.ShapeDtypeStruct((ROWS, 128),...]
    reshape x5 -> x1, local copies, waits for them, and re-layouts: 16.8 us -> 0.13 us  [body(): ct = cotangent[0].reshape(4, 4, 8, 16).transpose(0, 1, 3, 2).reshape(4, TOK)]
    reduce_scatter x1 -> x0, waiting for transfers between devices: 15.1 us -> none  [body(): lax.psum_scatter(jnp.where(inside[:, None], picked, 0.0).astype(jnp.bfloa...]
    all_to_all x1 -> x2, starting transfers between devices: 7.3 us -> 10.8 us  [swap(): return lax.all_to_all(x, axis, split_axis=0, concat_axis=0, tiled=True)]
  transfers between devices with their start and end apart: 3 -> 2, of which waited for: 3 -> 2; matrix products, arithmetic and copies ran while one was open for 3% -> 6% of each run, Pallas kernels for 0% -> 0%
where the time goes in v1:
time: 139 us; the launch traced here: 138 us
  blocking collectives  80.2 us (58%)
  Pallas kernels  19.6 us (14%)
  waiting for transfers between devices  11 us (8%)
  starting transfers between devices  10.8 us (8%)
  local copies, waits for them, and re-layouts  9.84 us (7%)
  other arithmetic  6.06 us (4%)
    all_to_all x4, blocking collectives, swap(): return lax.all_to_all(x, axis, split_axis=0, concat_axis=0, tiled=True)  80.2 us
    pallas_call x1, Pallas kernels, token_grads(): pl.pallas_call(token_kernel, out_shape=jax.ShapeDtypeStruct((ROWS, 128),...  16.8 us
    all_to_all x2, waiting for transfers between devices, swap(): return lax.all_to_all(x, axis, split_axis=0, concat_axis=0, tiled=True)  11 us
    all_to_all x2, starting transfers between devices, swap(): return lax.all_to_all(x, axis, split_axis=0, concat_axis=0, tiled=True)  10.8 us
    unnamed x22, local copies, waits for them, and re-layouts  3.23 us
    pallas_call x1, Pallas kernels, unpack(): pl.pallas_call(unpack_kernel, out_shape=(jax.ShapeDtypeStruct((128, HID),...  2.82 us
  transfers between devices with their start and end apart: 2, of which 2 were waited for; matrix products, arithmetic and copies ran while one was open for 6% of the time, Pallas kernels for 0%

profile of v1, /device:TPU:1, one launch (start us, length us, event | category | flops | bytes accessed | tf_op | source)
XLA Modules:
  0.0 138.4 jit_solution(2024308223003882059)
XLA Ops:
  0.6 0.0 copy-start
  0.6 0.8 and_reduce_fusion
  1.4 0.1 and.12
  1.5 0.7 fusion.6
  2.3 0.0 copy-done
  2.3 1.9 %gather_fusion.1 = bf16[256,128]{1,0:T(8,128)(2,1)S(1)} fusion(bf16[2,32,64,128]{3,2,1,0:T(8,128)(2,1)S(1)} %bitcast.28, s32[256]{0:T(256)S(1)} %bitcast.29), kind=kCustom, calls=%fused_computation.1 | custom fusion | bytes 134144 | tf_op jit(solution)/shard_map/gather | solution.py:234
  4.2 0.7 broadcast_select_fusion
  4.9 6.5 %all-to-all-start.1 = ((bf16[8,32,128]{2,1,0:T(8,128)(2,1)}), bf16[8,32,128]{2,1,0:T(8,128)(2,1)S(1)}, u32[]{:S(2)}, u32[]{:S(2)}) async-start(bf16[8,32,128]{2,1,0:T(8,128)(2,1)} %broadcast_select_fusion), calls=%async_computation.1 | async-start | bytes 131072 | tf_op jit(solution)/shard_map/all_to_all | solution.py:201
  11.4 0.7 fusion.2
  12.1 0.8 copy.23
  12.8 0.1 iota_compare_fusion
  12.9 0.1 broadcast_in_dim.47
  13.0 0.1 broadcast_in_dim.48
  13.1 0.1 copy.24
  13.2 0.1 reshape.196
  13.3 0.8 gather_fusion
  14.1 1.5 %bitcast_select_fusion = bf16[8,512,128]{2,1,0:T(8,128)(2,1)} fusion(pred[8,512]{1,0:T(8,128)(4,1)S(1)} %broadcast_in_dim.48, bf16[8,512,128]{2,1,0:T(8,128)(2,1)S(1)} %bitcast.32), kind=kLoop, calls=%fused_computation.2 | loop fusion | flops 524288 | bytes 2101248 | tf_op jit(solution)/shard_map/jit(_where)/select_n | solution.py:240
  15.7 0.0 copy-start.2
  15.7 0.6 all-to-all-done.1.qry_ref
  16.3 4.4 %all-to-all-start = ((bf16[8,512,128]{2,1,0:T(8,128)(2,1)}), bf16[8,512,128]{2,1,0:T(8,128)(2,1)S(1)}, u32[]{:S(2)}, u32[]{:S(2)}) async-start(bf16[8,512,128]{2,1,0:T(8,128)(2,1)} %bitcast_select_fusion), calls=%async_computation | async-start | bytes 2097152 | tf_op jit(solution)/shard_map/all_to_all | solution.py:201
  20.6 0.0 copy-done.6
  20.7 0.1 copy.25
  20.7 0.1 copy.26
  20.9 0.1 reshape.194
  21.0 0.0 copy-done.7
  21.0 0.0 copy-start.8
  21.0 0.6 pad.9.w_head
  21.6 0.6 pad.8.ct_ref
  22.2 0.0 copy-done.5
  22.2 0.8 copy.27
  23.0 0.0 copy-done.3
  23.0 0.9 copy.29
  23.9 0.0 copy-done.4
  23.9 0.0 copy-done.2
  23.9 1.3 copy.28
  25.2 10.4 %all-to-all-done.pat_ref = bf16[8,512,128]{2,1,0:T(8,128)(2,1)S(1)} async-done(((bf16[8,512,128]{2,1,0:T(8,128)(2,1)}), bf16[8,512,128]{2,1,0:T(8,128)(2,1)S(1)}, u32[]{:S(2)}, u32[]{:S(2)}) %all-to-all-start) | async-done | bytes 1048608 | tf_op jit(solution)/shard_map/all_to_all | solution.py:201
  35.6 0.0 copy-done.8
  35.6 0.9 broadcast_in_dim.54.gain_ref
  36.5 0.1 copy-done.1
  36.7 16.8 %token_grads.1 = bf16[5120,128]{1,0:T(8,128)(2,1)} custom-call(bf16[8,512,128]{2,1,0:T(8,128)(2,1)} %copy-done.1, bf16[8,32,128]{2,1,0:T(8,128)(2,1)} %copy-done.4, bf16[16,512]{1,0:T(8,128)(2,1)} %pad.8.ct_ref, bf16[384,128]{1,0:T(8,128)(2,1)} %bitcast.35, f32[384,128]{1,0:T(8,128)} %broadcast_in_dim.54.gain_ref, bf16[1152,384]{1,0:T(8,128)(2,1)} %bitcast.33, ...), custom_call_target="tpu_custom_call" | custom-call | tf_op jit(solution)/shard_map/token_grads/pallas_call | solution.py:147
  53.5 22.2 %all_to_all.44 = bf16[8,640,128]{2,1,0:T(8,128)(2,1)S(1)} all-to-all(bf16[8,640,128]{2,1,0:T(8,128)(2,1)} %bitcast.31), channel_id=1, replica_groups=mesh['dp'=32,'frame'=8] {'frame'}, dimensions={0} | all-to-all | bytes 2621440 | tf_op jit(solution)/shard_map/all_to_all | solution.py:201
  75.7 0.2 reduce_sum.24
  75.9 19.8 %all_to_all.45 = bf16[32,20,128]{2,1,0:T(8,128)(2,1)S(1)} all-to-all(bf16[32,20,128]{2,1,0:T(8,128)(2,1)S(1)} %all_to_all.33), channel_id=1, replica_groups=mesh['dp'=32,'frame'=8] {'dp'}, dimensions={0} | all-to-all | bytes 327680 | tf_op jit(solution)/shard_map/all_to_all | solution.py:201
  95.8 14.2 %all_to_all.46 = bf16[32,20,128]{2,1,0:T(8,128)(2,1)S(1)} all-to-all(bf16[32,20,128]{2,1,0:T(8,128)(2,1)S(1)} %tile.6), channel_id=1, replica_groups=mesh['dp'=32,'frame'=8] {'dp'}, dimensions={0} | all-to-all | bytes 327680 | tf_op jit(solution)/shard_map/all_to_all | solution.py:201
  110.0 0.2 tile.8
  110.2 24.1 %all_to_all.47 = bf16[8,640,128]{2,1,0:T(8,128)(2,1)} all-to-all(bf16[8,640,128]{2,1,0:T(8,128)(2,1)S(1)} %tile.8), channel_id=1, replica_groups=mesh['dp'=32,'frame'=8] {'frame'}, dimensions={0} | all-to-all | bytes 2621440 | tf_op jit(solution)/shard_map/all_to_all | solution.py:201
  134.3 2.8 %unpack.1 = (f32[128,384]{1,0:T(8,128)}, f32[1,384]{1,0:T(1,128)}, f32[384,1152]{1,0:T(8,128)}, f32[384,384]{1,0:T(8,128)}, f32[4,384]{1,0:T(4,128)}) custom-call(bf16[5120,128]{1,0:T(8,128)(2,1)} %bitcast.30), custom_call_target="tpu_custom_call" | custom-call | tf_op jit(solution)/shard_map/unpack/pallas_call | solution.py:184
  137.1 1.3 reduce.5
  (10 shorter events, 0.2 us)
Async XLA Ops:
  0.6 1.6 %copy-start = (bf16[1,2,32,64,128]{4,3,2,1,0:T(8,128)(2,1)S(1)}, bf16[1,2,32,64,128]{4,3,2,1,0:T(8,128)(2,1)}, u32[]{:S(2)}) copy-start(bf16[1,2,32,64,128]{4,3,2,1,0:T(8,128)(2,1)} %param.12) | copy-start | bytes 3145732
  4.9 11.3 %all-to-all-start.1 = ((bf16[8,32,128]{2,1,0:T(8,128)(2,1)}), bf16[8,32,128]{2,1,0:T(8,128)(2,1)S(1)}, u32[]{:S(2)}, u32[]{:S(2)}) async-start(bf16[8,32,128]{2,1,0:T(8,128)(2,1)} %broadcast_select_fusion), calls=%async_computation.1 | async-start | bytes 131072 | tf_op jit(solution)/shard_map/all_to_all | solution.py:201
  15.6 5.0 %copy-start.6 = (bf16[1,4,32,16]{2,3,1,0:T(8,128)(2,1)S(1)}, bf16[1,4,32,16]{2,3,1,0:T(8,128)(2,1)}, u32[]{:S(2)}) copy-start(bf16[1,4,32,16]{2,3,1,0:T(8,128)(2,1)} %param.18) | copy-start | bytes 12292
  15.6 5.3 %copy-start.7 = (bf16[4,384]{1,0:T(4,128)(2,1)S(1)}, bf16[4,384]{1,0:T(4,128)(2,1)}, u32[]{:S(2)}) copy-start(bf16[4,384]{1,0:T(4,128)(2,1)} %param.23) | copy-start | bytes 9220
  15.6 6.6 %copy-start.5 = (bf16[128,384]{1,0:T(8,128)(2,1)S(1)}, bf16[128,384]{1,0:T(8,128)(2,1)}, u32[]{:S(2)}) copy-start(bf16[128,384]{1,0:T(8,128)(2,1)} %param.19) | copy-start | bytes 294916
  15.6 7.3 %copy-start.3 = (bf16[384,384]{1,0:T(8,128)(2,1)S(1)}, bf16[384,384]{1,0:T(8,128)(2,1)}, u32[]{:S(2)}) copy-start(bf16[384,384]{1,0:T(8,128)(2,1)} %w_out.1) | copy-start | bytes 884740
  15.7 8.2 %copy-start.2 = (bf16[384,1152]{1,0:T(8,128)(2,1)S(1)}, bf16[384,1152]{1,0:T(8,128)(2,1)}, u32[]{:S(2)}) copy-start(bf16[384,1152]{1,0:T(8,128)(2,1)} %w_qkv.1) | copy-start | bytes 2654212
  16.3 7.6 %copy-start.4 = (bf16[8,32,128]{2,1,0:T(8,128)(2,1)}, bf16[8,32,128]{2,1,0:T(8,128)(2,1)S(1)}, u32[]{:S(2)}) copy-start(bf16[8,32,128]{2,1,0:T(8,128)(2,1)S(1)} %all-to-all-done.1.qry_ref) | copy-start | bytes 196612
  16.3 19.4 %all-to-all-start = ((bf16[8,512,128]{2,1,0:T(8,128)(2,1)}), bf16[8,512,128]{2,1,0:T(8,128)(2,1)S(1)}, u32[]{:S(2)}, u32[]{:S(2)}) async-start(bf16[8,512,128]{2,1,0:T(8,128)(2,1)} %bitcast_select_fusion), calls=%async_computation | async-start | bytes 2097152 | tf_op jit(solution)/shard_map/all_to_all | solution.py:201
  21.0 14.6 %copy-start.8 = (f32[384]{0:T(512)S(1)}, f32[384]{0:T(512)}, u32[]{:S(2)}) copy-start(f32[384]{0:T(512)} %param.20) | copy-start | bytes 4612
  35.6 1.1 copy-start.1

commit v2 on v1

--- a/solution.py
+++ b/solution.py
@@ -9,7 +9,7 @@
 SIZE = 48
 HID = 384
 TOK = 512
-ROWS = 5120
+HALF = 2560
 F32 = jnp.float32
 BF16 = jnp.bfloat16
 
@@ -22,32 +22,72 @@
 TN = ((0,), (0,))
 
 
+def gather_kernel(vis_ref, count_ref, qf_ref, qb_ref, qc_ref, feats_ref, out_ref):
+    base = lax.axis_index("frame") * 2
+    for g in range(16):
+        for fr in range(2):
+            shown = count_ref[0, g, fr]
+            for k in range(2):
+                at = (g // 2, pl.ds(((g % 2) * 2 + fr) * 128 + k * 64, 64))
+                tile = feats_ref[0, fr, vis_ref[0, g, fr, k]]
+                if k:
+                    tile = jnp.where(shown > k, tile, jnp.zeros_like(tile))
+                out_ref[at] = tile
+    local = qf_ref[...] - base
+    index = local * 2048 + qb_ref[...] * 64 + qc_ref[...]
+    index = jnp.where((local >= 0) & (local < 2), index, -1)
+    column = jnp.broadcast_to(index, (128, 256)).T[:, :1]
+    query = jnp.zeros((256, 128), F32)
+    for j in range(8):
+        lanes = lax.broadcasted_iota(jnp.int32, (256, 512), 1) + j * 512
+        chosen = jnp.where(lanes == column, 1.0, 0.0).astype(BF16)
+        rows = feats_ref[0, j // 4, (j % 4) * 8 : (j % 4) * 8 + 8].reshape(512, 128)
+        query = query + dot(chosen, rows)
+    out_ref[:, 512:544, :] = query.astype(BF16).reshape(8, 32, 128)
+
+
+def gather(vis_block, vis_count, query_frame, query_block, query_cell, features):
+    vm = pl.BlockSpec(memory_space=pltpu.VMEM)
+    sm = pl.BlockSpec(memory_space=pltpu.SMEM)
+    return pl.pallas_call(
+        gather_kernel,
+        out_shape=jax.ShapeDtypeStruct((8, 544, 128), BF16),
+        in_specs=[sm, sm, vm, vm, vm, vm],
+        out_specs=vm,
+        name="gather",
+    )(vis_block, vis_count, query_frame, query_block, query_cell, features)
+
+
 def token_kernel(
     pat_ref,
-    qry_ref,
     ct_ref,
     w_in_t,
-    gain_ref,
+    gain_in,
     w_qkv_t,
     w_qkv,
     w_out_t,
     w_out,
     w_head,
-    out_ref,
+    keep_ref,
+    send_ref,
     corr32,
     corr16,
     x_zero,
     normed,
-    hidden,
+    left,
     qkv,
-    mixed,
     d_y,
-    d_y16,
     d_mixed,
-    d_qkv,
+    right,
     inv_ref,
+    g_in_ref,
+    gain_ref,
 ):
-    query = jnp.sum(qry_ref[...].astype(F32), axis=0).astype(BF16)
+    hidden, mixed = left.at[0], left.at[1]
+    d_qkv, d_y16 = right.at[0:1152], right.at[1152:1536]
+    core = lax.axis_index("frame") % 2
+    gain_ref[...] = jnp.broadcast_to(gain_in[...], (128, HID)).T
+    query = jnp.sum(pat_ref[:, 512:544, :].astype(F32), axis=0).astype(BF16)
     scale = 128 ** (-0.5)
     for g in range(2):
         for s in range(8):
@@ -126,90 +166,118 @@
         m_two = jnp.mean(dn * nrm, axis=0, keepdims=True)
         dx = inv_ref[:1, cols] * (dn - m_one - nrm * m_two) + d_y[:, cols]
         g_in = g_in + dot(corr16[cols, :], dx.astype(BF16), ((0,), (1,)))
-    for j in range(9):
-        part = dot(hidden[...], d_qkv[j * 128 : j * 128 + 128, :], NT)
-        out_ref[j * 384 : j * 384 + 384, :] = part.astype(BF16)
-    for j in range(3):
-        part = dot(mixed[...], d_y16[j * 128 : j * 128 + 128, :], NT)
-        out_ref[3456 + j * 384 : 3456 + j * 384 + 384, :] = part.astype(BF16)
     gain_row = jnp.sum(gain_sum.T, axis=0, keepdims=True)
     at_four = lax.broadcasted_iota(jnp.int32, (16, HID), 0) == 4
     head = jnp.where(at_four, jnp.broadcast_to(gain_row, (16, HID)), head)
     for j in range(3):
-        lanes = slice(j * 128, j * 128 + 128)
-        out_ref[4608 + j * 128 : 4736 + j * 128, :] = g_in[:, lanes].astype(BF16)
-        out_ref[4992 + j * 16 : 5008 + j * 16, :] = head[:, lanes].astype(BF16)
-    out_ref[5040:ROWS, :] = jnp.zeros((ROWS - 5040, 128), BF16)
-
-
-def token_grads(pat, qry, ct, w_in_t, gain, w_qkv_t, w_qkv, w_out_t, w_out, w_head):
+        g_in_ref[j * 128 : j * 128 + 128, :] = g_in[:, j * 128 : j * 128 + 128]
+    for ref, half in ((keep_ref, core), (send_ref, 1 - core)):
+        for i in range(2):
+            j = half * 2 + i
+            rows = pl.ds(pl.multiple_of(j * HID, HID), HID)
+            part = dot(left[jnp.where(j == 3, 1, 0)], right[rows, :], NT)
+            for n in range(3):
+                at = (i * 3 + n) * HID
+                ref[at : at + HID, :] = part[:, n * 128 : n * 128 + 128].astype(BF16)
+        ref[2304:2496, :] = g_in_ref[pl.ds(pl.multiple_of(half * 192, 8), 192), :].astype(BF16)
+        part = jnp.where(half == 0, head, 0.0).astype(BF16)
+        for n in range(3):
+            ref[2496 + n * 16 : 2512 + n * 16, :] = part[:, n * 128 : n * 128 + 128]
+        ref[2544:HALF, :] = jnp.zeros((HALF - 2544, 128), BF16)
+
+
+def token_grads(pat, ct, w_in_t, gain, w_qkv_t, w_qkv, w_out_t, w_out, w_head):
     vm = pl.BlockSpec(memory_space=pltpu.VMEM)
+    half = jax.ShapeDtypeStruct((HALF, 128), BF16)
     return pl.pallas_call(
         token_kernel,
-        out_shape=jax.ShapeDtypeStruct((ROWS, 128), BF16),
-        in_specs=[vm] * 10,
-        out_specs=vm,
+        out_shape=(half, half),
+        in_specs=[vm] * 9,
+        out_specs=(vm, vm),
         scratch_shapes=[
             pltpu.VMEM((TOK, 128), F32),
             pltpu.VMEM((TOK, 128), BF16),
             pltpu.VMEM((HID, TOK), F32),
             pltpu.VMEM((HID, TOK), F32),
-            pltpu.VMEM((HID, TOK), BF16),
+            pltpu.VMEM((2, HID, TOK), BF16),
             pltpu.VMEM((3 * HID, TOK), BF16),
-            pltpu.VMEM((HID, TOK), BF16),
             pltpu.VMEM((HID, TOK), F32),
             pltpu.VMEM((HID, TOK), BF16),
-            pltpu.VMEM((HID, TOK), BF16),
-            pltpu.VMEM((3 * HID, TOK), BF16),
+            pltpu.VMEM((4 * HID, TOK), BF16),
             pltpu.VMEM((8, TOK), F32),
+            pltpu.VMEM((HID, 128), F32),
+            pltpu.VMEM((HID, 128), F32),
         ],
         name="token_grads",
-    )(pat, qry, ct, w_in_t, gain, w_qkv_t, w_qkv, w_out_t, w_out, w_head)
-
-
-def unpack_kernel(x_ref, g_in, g_gain, g_qkv, g_out, g_head):
-    for j in range(9):
-        g_qkv[:, j * 128 : j * 128 + 128] = x_ref[j * 384 : j * 384 + 384, :].astype(F32)
-    for j in range(3):
-        lanes = slice(j * 128, j * 128 + 128)
-        g_out[:, lanes] = x_ref[3456 + j * 384 : 3840 + j * 384, :].astype(F32)
-        g_in[:, lanes] = x_ref[4608 + j * 128 : 4736 + j * 128, :].astype(F32)
-        tail = x_ref[4992 + j * 16 : 5008 + j * 16, :].astype(F32)
-        g_head[:, lanes] = tail[:4]
-        g_gain[:, lanes] = tail[4:5]
-
-
-def unpack(x):
+    )(pat, ct, w_in_t, gain, w_qkv_t, w_qkv, w_out_t, w_out, w_head)
+
+
+def unpack_kernel(own_ref, other_ref, g_in, g_gain, g_qkv, g_out, g_head):
+    core = lax.axis_index("frame") % 2
+
+    def write(low, high):
+        for j in range(3):
+            lanes = slice(j * 128, j * 128 + 128)
+            first, second = slice(j * HID, j * HID + HID), slice((j + 3) * HID, (j + 4) * HID)
+            g_qkv[:, lanes] = low[first, :].astype(F32)
+            g_qkv[:, HID + j * 128 : HID + j * 128 + 128] = low[second, :].astype(F32)
+            g_qkv[:, 2 * HID + j * 128 : 2 * HID + j * 128 + 128] = high[first, :].astype(F32)
+            g_out[:, lanes] = high[second, :].astype(F32)
+            tail = low[2496 + j * 16 : 2512 + j * 16, :].astype(F32)
+            g_head[:, lanes] = tail[:4]
+            g_gain[lanes] = tail[4]
+        g_in[:, 0:128] = low[2304:2432, :].astype(F32)
+        g_in[0:64, 128:256] = low[2432:2496, :].astype(F32)
+        g_in[64:128, 128:256] = high[2304:2368, :].astype(F32)
+        g_in[:, 256:384] = high[2368:2496, :].astype(F32)
+
+    @pl.when(core == 0)
+    def _():
+        write(own_ref, other_ref)
+
+    @pl.when(core == 1)
+    def _():
+        write(other_ref, own_ref)
+
+
+def unpack(own, other):
     vm = pl.BlockSpec(memory_space=pltpu.VMEM)
-    g_in, g_gain, g_qkv, g_out, g_head = pl.pallas_call(
+    return pl.pallas_call(
         unpack_kernel,
         out_shape=(
             jax.ShapeDtypeStruct((128, HID), F32),
-            jax.ShapeDtypeStruct((1, HID), F32),
+            jax.ShapeDtypeStruct((HID,), F32),
             jax.ShapeDtypeStruct((HID, 3 * HID), F32),
             jax.ShapeDtypeStruct((HID, HID), F32),
             jax.ShapeDtypeStruct((4, HID), F32),
         ),
-        in_specs=[vm],
+        in_specs=[vm, vm],
         out_specs=(vm,) * 5,
         name="unpack",
-    )(x)
-    return g_in, g_gain.reshape(HID), g_qkv, g_out, g_head
-
-
-def swap(x, axis):
-    return lax.all_to_all(x, axis, split_axis=0, concat_axis=0, tiled=True)
+    )(own, other)
+
+
+Y_GROUPS = [[0, 2, 4, 6], [1, 3, 5, 7]]
+PARTNER = [(i, i ^ 1) for i in range(8)]
+
+
+def swap(x, axis, groups=None):
+    return lax.all_to_all(
+        x, axis, split_axis=0, concat_axis=0, axis_index_groups=groups, tiled=True
+    )
 
 
 def fold(x, n):
     return jnp.sum(x.reshape(n, x.shape[0] // n, x.shape[1]).astype(F32), axis=0).astype(BF16)
 
 
-def sum_all(x):
-    x = fold(swap(x, "frame"), 8)
+def sum_all(keep, send):
+    x = (keep.astype(F32) + lax.ppermute(send, "frame", PARTNER).astype(F32)).astype(BF16)
+    x = fold(swap(x, "frame", Y_GROUPS), 4)
     x = fold(swap(x, "dp"), 32)
     x = swap(jnp.tile(x, (32, 1)), "dp")
-    return swap(jnp.tile(x, (8, 1)), "frame")
+    x = swap(jnp.tile(x, (4, 1)), "frame", Y_GROUPS)
+    return x, lax.ppermute(x, "frame", PARTNER)
 
 
 def body(
@@ -226,34 +294,22 @@
     w_out,
     w_head,
 ):
-    feats = features[0]
-    fr_dev = feats.shape[0]
-    frame_pos = lax.axis_index("frame")
-    local = query_frame[0] - frame_pos * fr_dev
-    inside = (local >= 0) & (local < fr_dev)
-    picked = feats[jnp.clip(local, 0, fr_dev - 1), query_block[0], query_cell[0]]
-    picked = jnp.where(inside[:, None], picked, jnp.zeros((), BF16))
-    queries = swap(picked, "frame").reshape(8, 32, 128)
-    frame_ids = jnp.arange(fr_dev, dtype=jnp.int32)[None, :, None]
-    patches = feats[frame_ids, vis_block[0]]
-    live = jnp.arange(2, dtype=jnp.int32)[None, None, :] < vis_count[0][:, :, None]
-    patches = jnp.where(live[..., None, None], patches, jnp.zeros((), BF16))
-    arrived = swap(patches.reshape(16 * 256, 128), "frame").reshape(8, 512, 128)
+    outgoing = gather(vis_block, vis_count, query_frame, query_block, query_cell, features)
+    arrived = swap(outgoing, "frame")
     ct = cotangent[0].reshape(4, 4, 8, 16).transpose(0, 1, 3, 2).reshape(4, TOK)
     ct = jnp.pad(ct, ((0, 12), (0, 0)))
-    packed = token_grads(
+    keep, send = token_grads(
         arrived,
-        queries,
         ct,
         w_in.T,
-        jnp.broadcast_to(gain[:, None], (HID, 128)),
+        gain.reshape(1, HID),
         w_qkv.T,
         w_qkv,
         w_out.T,
         w_out,
         jnp.pad(w_head, ((0, 12), (0, 0))),
     )
-    return unpack(sum_all(packed))
+    return unpack(*sum_all(keep, send))
 
 
 def solution(mesh):

time: 139 us -> 118 us (0.85)
  blocking collectives: 80.2 us -> 56.3 us
  other arithmetic: 6.06 us -> 1.43 us
  waiting for transfers between devices: 11 us -> 14.3 us
  Pallas kernels: 19.6 us -> 22.4 us
  starting transfers between devices: 10.8 us -> 12.7 us
    all_to_all x4, blocking collectives: 80.2 us -> 56.3 us  [swap(): lax.all_to_all(x, axis, split_axis=0, concat_axis=0, axis_index_groups=gr...]
    ppermute x0 -> x2, starting transfers between devices: none -> 5.92 us  [the longest x1 4.96 us: sum_all(): return (x, lax.ppermute(x, 'frame', PARTNER))]
    unnamed x22 -> x24, local copies, waits for them, and re-layouts: 3.23 us -> 7.65 us
    all_to_all x2 -> x1, starting transfers between devices: 10.8 us -> 6.8 us  [swap(): lax.all_to_all(x, axis, split_axis=0, concat_axis=0, axis_index_groups=gr...]
    ppermute x0 -> x2, waiting for transfers between devices: none -> 3.66 us  [the longest x1 1.93 us: sum_all(): lax.ppermute(send, 'frame', PARTNER).astype(F32)]
    gather x2 -> x0, local copies, waits for them, and re-layouts: 2.73 us -> none  [the longest x1 1.93 us: body(): feats[jnp.clip(local, 0, fr_dev - 1), query_block[0], query_cell[0]]]
    pallas_call x1 -> x2, Pallas kernels: 16.8 us -> 19.4 us  [the longest x1 16.1 us: token_grads(): pl.pallas_call(token_kernel, out_shape=(half, half), in_specs=[vm] * 9, o...]
    select_n x2 -> x0, other arithmetic: 2.24 us -> none  [the longest x1 1.51 us: body(): patches = jnp.where(live[..., None, None], patches, jnp.zeros((), BF16))]
  transfers between devices with their start and end apart: 2 -> 3, of which waited for: 2 -> 3; matrix products, arithmetic and copies ran while one was open for 6% -> 4% of each run, Pallas kernels for 0% -> 0%
where the time goes in v2:
time: 118 us
  blocking collectives  56.3 us (48%)
  Pallas kernels  22.4 us (19%)
  waiting for transfers between devices  14.3 us (12%)
  starting transfers between devices  12.7 us (11%)
  local copies, waits for them, and re-layouts  9.84 us (8%)
  other arithmetic  1.43 us (1%)
    all_to_all x4, blocking collectives, swap(): lax.all_to_all(x, axis, split_axis=0, concat_axis=0, axis_index_groups=gr...  56.3 us
    pallas_call x1, Pallas kernels, token_grads(): pl.pallas_call(token_kernel, out_shape=(half, half), in_specs=[vm] * 9, o...  16.1 us
    all_to_all x1, waiting for transfers between devices, swap(): lax.all_to_all(x, axis, split_axis=0, concat_axis=0, axis_index_groups=gr...  10.6 us
    unnamed x24, local copies, waits for them, and re-layouts  7.65 us
    all_to_all x1, starting transfers between devices, swap(): lax.all_to_all(x, axis, split_axis=0, concat_axis=0, axis_index_groups=gr...  6.8 us
    ppermute x1, starting transfers between devices, sum_all(): return (x, lax.ppermute(x, 'frame', PARTNER))  4.96 us
    pallas_call x1, Pallas kernels, gather(): pl.pallas_call(gather_kernel, out_shape=jax.ShapeDtypeStruct((8, 544, 128...  3.31 us
    pallas_call x1, Pallas kernels, unpack(): pl.pallas_call(unpack_kernel, out_shape=(jax.ShapeDtypeStruct((128, HID),...  2.92 us
  transfers between devices with their start and end apart: 3, of which 3 were waited for; matrix products, arithmetic and copies ran while one was open for 4% of the time, Pallas kernels for 0%

profile of v2, /device:TPU:1, one launch (start us, length us, event | category | flops | bytes accessed | tf_op | source)
XLA Modules:
  0.0 117.7 jit_solution(10187119359644452333)
XLA Ops:
  0.6 1.4 %copy.24.count_ref = s32[1,16,2]{2,1,0:T(8,128)} copy(s32[1,16,2]{1,2,0:T(2,128)} %param.14) | data formatting | bytes 256 | tf_op args[2]
  2.0 1.4 %copy.23.vis_ref = s32[1,16,2,2]{3,2,1,0:T(2,128)} copy(s32[1,16,2,2]{1,3,2,0:T(2,128)} %param.13) | data formatting | bytes 512 | tf_op args[1]
  3.4 3.3 %gather.1 = bf16[8,544,128]{2,1,0:T(8,128)(2,1)} custom-call(s32[1,16,2,2]{3,2,1,0:T(2,128)} %copy.23.vis_ref, s32[1,16,2]{2,1,0:T(8,128)} %copy.24.count_ref, s32[1,256]{1,0:T(1,128)} %qf_ref.1, s32[1,256]{1,0:T(1,128)} %qb_ref.1, s32[1,256]{1,0:T(1,128)} %qc_ref.1, bf16[1,2,32,64,128]{4,3,2,1,0:T(8,128)(2,1)} %feats_ref.1), custom_call_target="tpu_custom_call" | custom-call | tf_op jit(solution)/shard_map/gather/pallas_call | solution.py:52
  6.7 0.0 copy-start.8
  6.7 0.0 copy-start.6
  6.7 0.0 copy-start.7
  6.7 0.0 copy-start.5
  6.7 0.0 copy-start.3
  6.7 0.0 copy-start.1
  6.7 6.8 %all-to-all-start = ((bf16[8,544,128]{2,1,0:T(8,128)(2,1)}), bf16[8,544,128]{2,1,0:T(8,128)(2,1)S(1)}, u32[]{:S(2)}, u32[]{:S(2)}) async-start(bf16[8,544,128]{2,1,0:T(8,128)(2,1)} %gather.1), calls=%async_computation | async-start | bytes 2228224 | tf_op jit(solution)/shard_map/all_to_all | solution.py:265
  13.5 0.0 copy-done.8
  13.5 0.6 reshape.40.gain_in
  14.1 0.0 copy-done.6
  14.1 0.1 copy.25
  14.2 0.1 copy.26
  14.3 0.1 reshape.39
  14.4 0.0 copy-done.7
  14.4 0.6 pad.9.w_head
  15.0 0.6 pad.8.ct_ref
  15.6 0.0 copy-done.5
  15.6 0.8 copy.27
  16.4 0.0 copy-done.3
  16.4 0.9 copy.29
  17.3 0.0 copy-done.1
  17.3 1.3 %copy.28 = bf16[384,1152]{0,1:T(8,128)(2,1)} copy(bf16[384,1152]{1,0:T(8,128)(2,1)S(1)} %copy-done.1) | data formatting | bytes 1769472 | tf_op args[9]
  18.6 10.6 %all-to-all-done.pat_ref = bf16[8,544,128]{2,1,0:T(8,128)(2,1)S(1)} async-done(((bf16[8,544,128]{2,1,0:T(8,128)(2,1)}), bf16[8,544,128]{2,1,0:T(8,128)(2,1)S(1)}, u32[]{:S(2)}, u32[]{:S(2)}) %all-to-all-start) | async-done | bytes 1114144 | tf_op jit(solution)/shard_map/all_to_all | solution.py:265
  29.2 0.0 copy-start
  29.2 1.0 copy-done
  30.2 16.1 %token_grads.1 = (bf16[2560,128]{1,0:T(8,128)(2,1)}, bf16[2560,128]{1,0:T(8,128)(2,1)}) custom-call(bf16[8,544,128]{2,1,0:T(8,128)(2,1)} %copy-done, bf16[16,512]{1,0:T(8,128)(2,1)} %pad.8.ct_ref, bf16[384,128]{1,0:T(8,128)(2,1)} %bitcast.15, f32[1,384]{1,0:T(1,128)} %reshape.40.gain_in, bf16[1152,384]{1,0:T(8,128)(2,1)} %bitcast.10, ...), custom_call_target="tpu_custom_call" | custom-call | tf_op jit(solution)/shard_map/token_grads/pallas_call | solution.py:192
  46.3 1.0 collective-permute-start
  47.3 1.9 %collective-permute-done = bf16[2560,128]{1,0:T(8,128)(2,1)S(1)} collective-permute-done((bf16[2560,128]{1,0:T(8,128)(2,1)}, bf16[2560,128]{1,0:T(8,128)(2,1)S(1)}, u32[]{:S(2)}, u32[]{:S(2)}) %collective-permute-start) | collective-permute-done | bytes 655392 | tf_op jit(solution)/shard_map/ppermute | solution.py:275
  49.2 1.3 %add_convert_fusion = bf16[2560,128]{1,0:T(8,128)(2,1)S(1)} fusion(bf16[2560,128]{1,0:T(8,128)(2,1)S(1)} %collective-permute-done, bf16[2560,128]{1,0:T(8,128)(2,1)} %get-tuple-element.7), kind=kLoop, calls=%fused_computation | loop fusion | flops 1310720 | bytes 1966080 | tf_op jit(solution)/shard_map/convert_element_type | solution.py:275
  50.5 13.0 %all_to_all.37 = bf16[4,640,128]{2,1,0:T(8,128)(2,1)S(1)} all-to-all(bf16[4,640,128]{2,1,0:T(8,128)(2,1)S(1)} %bitcast.13), channel_id=1, replica_groups={{0,2,4,6},{1,3,5,7},{8,10,12,14},{9,11,13,15},{16,18,20,22},{17,19,21,2..., dimensions={0} | all-to-all | bytes 1310720 | tf_op jit(solution)/shard_map/all_to_all | solution.py:265
  63.5 0.1 reduce_sum.24
  63.7 19.5 %all_to_all.38 = bf16[32,20,128]{2,1,0:T(8,128)(2,1)S(1)} all-to-all(bf16[32,20,128]{2,1,0:T(8,128)(2,1)S(1)} %all_to_all.27), channel_id=1, replica_groups=mesh['dp'=32,'frame'=8] {'dp'}, dimensions={0} | all-to-all | bytes 327680 | tf_op jit(solution)/shard_map/all_to_all | solution.py:265
  83.3 13.8 %all_to_all.39 = bf16[32,20,128]{2,1,0:T(8,128)(2,1)S(1)} all-to-all(bf16[32,20,128]{2,1,0:T(8,128)(2,1)S(1)} %tile.6), channel_id=1, replica_groups=mesh['dp'=32,'frame'=8] {'dp'}, dimensions={0} | all-to-all | bytes 327680 | tf_op jit(solution)/shard_map/all_to_all | solution.py:265
  97.1 0.1 tile.8
  97.2 10.0 %all_to_all.40 = bf16[4,640,128]{2,1,0:T(8,128)(2,1)S(1)} all-to-all(bf16[4,640,128]{2,1,0:T(8,128)(2,1)S(1)} %tile.8), channel_id=1, replica_groups={{0,2,4,6},{1,3,5,7},{8,10,12,14},{9,11,13,15},{16,18,20,22},{17,19,21,2..., dimensions={0} | all-to-all | bytes 1310720 | tf_op jit(solution)/shard_map/all_to_all | solution.py:265
  107.2 0.0 copy-start.2
  107.2 5.0 %collective-permute-start.1 = (bf16[2560,128]{1,0:T(8,128)(2,1)S(1)}, bf16[2560,128]{1,0:T(8,128)(2,1)S(1)}, u32[]{:S(2)}, u32[]{:S(2)}) collective-permute-start(bf16[2560,128]{1,0:T(8,128)(2,1)S(1)} %bitcast.11), channel_id=1, source_target_pairs={{0,1},{1,0},{2,3},{3,2},{4,5},{5,4},{6,7},{7,6},{8,9},{9,8},{10,11... | collective-permute-start | bytes 1966088 | tf_op jit(solution)/shard_map/ppermute | solution.py:280
  112.2 1.7 %collective-permute-done.1.other_ref = bf16[2560,128]{1,0:T(8,128)(2,1)S(1)} collective-permute-done((bf16[2560,128]{1,0:T(8,128)(2,1)S(1)}, bf16[2560,128]{1,0:T(8,128)(2,1)S(1)}, u32[]{:S(2)}, u32[]{:S(2)}) %collective-permute-start.1) | collective-permute-done | bytes 655392 | tf_op jit(solution)/shard_map/ppermute | solution.py:280
  113.9 0.0 copy-done.2
  113.9 0.0 copy-start.4
  113.9 0.8 copy-done.4
  114.8 2.9 %unpack.1 = (f32[128,384]{1,0:T(8,128)}, f32[384]{0:T(512)}, f32[384,1152]{1,0:T(8,128)}, f32[384,384]{1,0:T(8,128)}, f32[4,384]{1,0:T(4,128)}) custom-call(bf16[2560,128]{1,0:T(8,128)(2,1)} %bitcast.12, bf16[2560,128]{1,0:T(8,128)(2,1)} %copy-done.4), custom_call_target="tpu_custom_call" | custom-call | tf_op jit(solution)/shard_map/unpack/pallas_call | solution.py:245
  (4 shorter events, 0.2 us)
Async XLA Ops:
  6.7 6.9 %copy-start.8 = (f32[384]{0:T(512)S(1)}, f32[384]{0:T(512)}, u32[]{:S(2)}) copy-start(f32[384]{0:T(512)} %param.20) | copy-start | bytes 4612
  6.7 7.4 %copy-start.6 = (bf16[1,4,32,16]{2,3,1,0:T(8,128)(2,1)S(1)}, bf16[1,4,32,16]{2,3,1,0:T(8,128)(2,1)}, u32[]{:S(2)}) copy-start(bf16[1,4,32,16]{2,3,1,0:T(8,128)(2,1)} %param.18) | copy-start | bytes 12292
  6.7 7.7 %copy-start.7 = (bf16[4,384]{1,0:T(4,128)(2,1)S(1)}, bf16[4,384]{1,0:T(4,128)(2,1)}, u32[]{:S(2)}) copy-start(bf16[4,384]{1,0:T(4,128)(2,1)} %param.23) | copy-start | bytes 9220
  6.7 9.0 %copy-start.5 = (bf16[128,384]{1,0:T(8,128)(2,1)S(1)}, bf16[128,384]{1,0:T(8,128)(2,1)}, u32[]{:S(2)}) copy-start(bf16[128,384]{1,0:T(8,128)(2,1)} %param.19) | copy-start | bytes 294916
  6.7 9.7 %copy-start.3 = (bf16[384,384]{1,0:T(8,128)(2,1)S(1)}, bf16[384,384]{1,0:T(8,128)(2,1)}, u32[]{:S(2)}) copy-start(bf16[384,384]{1,0:T(8,128)(2,1)} %w_out.1) | copy-start | bytes 884740
  6.7 10.6 %copy-start.1 = (bf16[384,1152]{1,0:T(8,128)(2,1)S(1)}, bf16[384,1152]{1,0:T(8,128)(2,1)}, u32[]{:S(2)}) copy-start(bf16[384,1152]{1,0:T(8,128)(2,1)} %w_qkv.1) | copy-start | bytes 2654212
  6.7 22.5 %all-to-all-start = ((bf16[8,544,128]{2,1,0:T(8,128)(2,1)}), bf16[8,544,128]{2,1,0:T(8,128)(2,1)S(1)}, u32[]{:S(2)}, u32[]{:S(2)}) async-start(bf16[8,544,128]{2,1,0:T(8,128)(2,1)} %gather.1), calls=%async_computation | async-start | bytes 2228224 | tf_op jit(solution)/shard_map/all_to_all | solution.py:265
  29.2 1.0 copy-start
  46.3 2.9 %collective-permute-start = (bf16[2560,128]{1,0:T(8,128)(2,1)}, bf16[2560,128]{1,0:T(8,128)(2,1)S(1)}, u32[]{:S(2)}, u32[]{:S(2)}) collective-permute-start(bf16[2560,128]{1,0:T(8,128)(2,1)} %get-tuple-element.8), channel_id=1, source_target_pairs={{0,1},{1,0},{2,3},{3,2},{4,5},{5,4},{6,7},{7,6},{8,9},{9,8},{10,11... | collective-permute-start | bytes 1966088 | tf_op jit(solution)/shard_map/ppermute | solution.py:275
  107.2 6.7 %copy-start.2 = (bf16[4,640,128]{2,1,0:T(8,128)(2,1)}, bf16[4,640,128]{2,1,0:T(8,128)(2,1)S(1)}, u32[]{:S(2)}) copy-start(bf16[4,640,128]{2,1,0:T(8,128)(2,1)S(1)} %all_to_all.40) | copy-start | bytes 1966084
  107.2 6.7 %collective-permute-start.1 = (bf16[2560,128]{1,0:T(8,128)(2,1)S(1)}, bf16[2560,128]{1,0:T(8,128)(2,1)S(1)}, u32[]{:S(2)}, u32[]{:S(2)}) collective-permute-start(bf16[2560,128]{1,0:T(8,128)(2,1)S(1)} %bitcast.11), channel_id=1, source_target_pairs={{0,1},{1,0},{2,3},{3,2},{4,5},{5,4},{6,7},{7,6},{8,9},{9,8},{10,11... | collective-permute-start | bytes 1966088 | tf_op jit(solution)/shard_map/ppermute | solution.py:280
  113.9 0.8 copy-start.4

commit v3 on v2

--- a/solution.py
+++ b/solution.py
@@ -26,10 +26,10 @@
     base = lax.axis_index("frame") * 2
     for g in range(16):
         for fr in range(2):
-            shown = count_ref[0, g, fr]
+            shown = count_ref[0, fr, g]
             for k in range(2):
                 at = (g // 2, pl.ds(((g % 2) * 2 + fr) * 128 + k * 64, 64))
-                tile = feats_ref[0, fr, vis_ref[0, g, fr, k]]
+                tile = feats_ref[0, fr, vis_ref[0, fr, k, g]]
                 if k:
                     tile = jnp.where(shown > k, tile, jnp.zeros_like(tile))
                 out_ref[at] = tile
@@ -55,13 +55,13 @@
         in_specs=[sm, sm, vm, vm, vm, vm],
         out_specs=vm,
         name="gather",
-    )(vis_block, vis_count, query_frame, query_block, query_cell, features)
+    )(vis_block.transpose(0, 2, 3, 1), vis_count.transpose(0, 2, 1), query_frame, query_block, query_cell, features)
 
 
 def token_kernel(
     pat_ref,
     ct_ref,
-    w_in_t,
+    w_in,
     gain_in,
     w_qkv_t,
     w_qkv,
@@ -82,6 +82,10 @@
     inv_ref,
     g_in_ref,
     gain_ref,
+    s_ref,
+    t_ref,
+    p_ref,
+    d_ref,
 ):
     hidden, mixed = left.at[0], left.at[1]
     d_qkv, d_y16 = right.at[0:1152], right.at[1152:1536]
@@ -99,86 +103,108 @@
     corr16[...] = corr32[...].astype(BF16)
 
     ct = ct_ref[...]
+    gain = gain_ref[...]
     for c in range(2):
-        cols = slice(c * 256, c * 256 + 256)
-        x0 = dot(w_in_t[...], corr16[cols, :], NT)
-        x_zero[:, cols] = x0
-        mean = jnp.mean(x0, axis=0, keepdims=True)
-        centred = x0 - mean
-        inv = lax.rsqrt(jnp.mean(centred * centred, axis=0, keepdims=True) + 1e-05)
-        nrm = centred * inv
-        inv_ref[:, cols] = jnp.broadcast_to(inv, (8, 256))
-        normed[:, cols] = nrm
-        hid = (nrm * gain_ref[:, :1]).astype(BF16)
-        hidden[:, cols] = hid
+        wide = slice(c * 256, c * 256 + 256)
+        dy = dot(w_head[...], ct[:, wide], TN)
+        d_y[:, wide] = dy
+        d_y16[:, wide] = dy.astype(BF16)
+        d_mixed[:, wide] = dot(w_out[...], d_y16[:, wide]).astype(BF16)
+        x_zero[:, wide] = dot(w_in[...], corr16[wide, :], ((0,), (1,)))
+        for n in range(2):
+            cols = slice(c * 256 + n * 128, c * 256 + n * 128 + 128)
+            x0 = x_zero[:, cols]
+            centred = x0 - jnp.mean(x0, axis=0, keepdims=True)
+            inv = lax.rsqrt(jnp.mean(centred * centred, axis=0, keepdims=True) + 1e-05)
+            inv_ref[:, cols] = jnp.broadcast_to(inv, (8, 128))
+            nrm = centred * inv
+            normed[:, cols] = nrm
+            hidden[:, cols] = (nrm * gain).astype(BF16)
         for r in range(3):
             rows = slice(r * 384, r * 384 + 384)
-            qkv[rows, cols] = dot(w_qkv_t[rows, :], hid).astype(BF16)
-        dy = dot(w_head[...], ct[:, cols], TN)
-        d_y[:, cols] = dy
-        dy16 = dy.astype(BF16)
-        d_y16[:, cols] = dy16
-        d_mixed[:, cols] = dot(w_out[...], dy16).astype(BF16)
+            qkv[rows, wide] = dot(w_qkv_t[rows, :], hidden[:, wide]).astype(BF16)
 
     own = (
         lax.broadcasted_iota(jnp.int32, (8, 128), 0)
         == lax.broadcasted_iota(jnp.int32, (8, 128), 1) % 8
     ).astype(F32)
     a_scale = SIZE ** (-0.5)
+    e_scale = a_scale * 1.4426950408889634
 
     def block(b, carry):
-        cols = pl.ds(pl.multiple_of(b * 128, 128), 128)
-        for h in range(HEADS):
-            rq = slice(h * SIZE, h * SIZE + SIZE)
-            rk = slice(HID + h * SIZE, HID + h * SIZE + SIZE)
-            rv = slice(2 * HID + h * SIZE, 2 * HID + h * SIZE + SIZE)
-            q_t, k_t, v_t = qkv[rq, cols], qkv[rk, cols], qkv[rv, cols]
-            d_a = d_mixed[rq, cols]
-            score = dot(k_t, q_t, TN).reshape(16, 8, 128) * a_scale
-            expo = jnp.exp(score - jnp.max(score, axis=0, keepdims=True))
+        def cols(h):
+            return pl.ds(pl.multiple_of((b * 2 + h // HEADS) * 128, 128), 128)
+
+        def rows(h, n):
+            at = n * HID + h % HEADS * SIZE
+            return slice(at, at + SIZE)
+
+        def scores(h):
+            s_ref[h] = dot(qkv[rows(h, 1), cols(h)], qkv[rows(h, 0), cols(h)], TN)
+            t_ref[h] = dot(qkv[rows(h, 2), cols(h)], d_mixed[rows(h, 0), cols(h)], TN).astype(BF16)
+
+        def weights(h):
+            score = s_ref[h].reshape(16, 8, 128)
+            expo = jnp.exp2((score - jnp.max(score, axis=0, keepdims=True)) * e_scale)
             prob = expo * (own / jnp.sum(expo, axis=0))[None]
-            prob16 = prob.reshape(128, 128).astype(BF16)
-            mixed[rq, cols] = dot(v_t, prob16).astype(BF16)
-            d_p = dot(v_t, d_a, TN).astype(BF16).astype(F32).reshape(16, 8, 128)
+            p_ref[h] = prob.reshape(128, 128).astype(BF16)
+            d_p = t_ref[h].astype(F32).reshape(16, 8, 128)
             inner = jnp.sum(d_p * prob, axis=0, keepdims=True)
-            d_s = (prob * (d_p - inner) * a_scale).reshape(128, 128).astype(BF16)
-            d_qkv[rq, cols] = dot(k_t, d_s).astype(BF16)
-            d_qkv[rk, cols] = dot(q_t, d_s, NT).astype(BF16)
-            d_qkv[rv, cols] = dot(d_a, prob16, NT).astype(BF16)
+            d_ref[h] = (prob * (d_p - inner)).reshape(128, 128).astype(BF16)
+
+        def products(h):
+            prob, d_s = p_ref[h], d_ref[h]
+            mixed[rows(h, 0), cols(h)] = dot(qkv[rows(h, 2), cols(h)], prob).astype(BF16)
+            d_v = dot(d_mixed[rows(h, 0), cols(h)], prob, NT)
+            d_q = dot(qkv[rows(h, 1), cols(h)], d_s) * a_scale
+            d_k = dot(qkv[rows(h, 0), cols(h)], d_s, NT) * a_scale
+            d_qkv[rows(h, 0), cols(h)] = d_q.astype(BF16)
+            d_qkv[rows(h, 1), cols(h)] = d_k.astype(BF16)
+            d_qkv[rows(h, 2), cols(h)] = d_v.astype(BF16)
+
+        for h in range(2 * HEADS + 2):
+            if h < 2 * HEADS:
+                scores(h)
+            if 1 <= h <= 2 * HEADS:
+                weights(h - 1)
+            if h >= 2:
+                products(h - 2)
         return carry
 
-    lax.fori_loop(0, 4, block, 0)
+    lax.fori_loop(0, 2, block, 0)
+
+    def pair_grads(ref, half, i):
+        j = half * 2 + i
+        rows = pl.ds(pl.multiple_of(j * HID, HID), HID)
+        part = dot(left[jnp.where(j == 3, 1, 0)], right[rows, :], NT)
+        for n in range(3):
+            at = (i * 3 + n) * HID
+            ref[at : at + HID, :] = part[:, n * 128 : n * 128 + 128].astype(BF16)
 
     head = jnp.zeros((16, HID), F32)
     gain_sum = jnp.zeros((HID, 128), F32)
-    g_in = jnp.zeros((128, HID), F32)
     for c in range(2):
-        cols = slice(c * 256, c * 256 + 256)
-        y16 = (x_zero[:, cols] + dot(w_out_t[...], mixed[:, cols])).astype(BF16)
-        head = head + dot(ct[:, cols], y16, NT)
-        dh = dot(w_qkv[...], d_qkv[:, cols])
-        nrm = normed[:, cols]
-        prod = dh * nrm
-        gain_sum = gain_sum + prod[:, :128] + prod[:, 128:]
-        gain = gain_ref[:, :1]
-        dn = dh * gain
-        m_one = jnp.mean(dn, axis=0, keepdims=True)
-        m_two = jnp.mean(dn * nrm, axis=0, keepdims=True)
-        dx = inv_ref[:1, cols] * (dn - m_one - nrm * m_two) + d_y[:, cols]
-        g_in = g_in + dot(corr16[cols, :], dx.astype(BF16), ((0,), (1,)))
+        wide = slice(c * 256, c * 256 + 256)
+        y16 = (x_zero[:, wide] + dot(w_out_t[...], mixed[:, wide])).astype(BF16)
+        head = head + dot(ct[:, wide], y16, NT)
+        x_zero[:, wide] = dot(w_qkv[...], d_qkv[:, wide])
+        for n in range(2):
+            cols = slice(c * 256 + n * 128, c * 256 + n * 128 + 128)
+            pair_grads(*((send_ref, 1 - core, n), (keep_ref, core, n))[c])
+            dh, nrm = x_zero[:, cols], normed[:, cols]
+            gain_sum = gain_sum + dh * nrm
+            dn = dh * gain
+            m_one = jnp.mean(dn, axis=0, keepdims=True)
+            m_two = jnp.mean(dn * nrm, axis=0, keepdims=True)
+            dx = inv_ref[:1, cols] * (dn - m_one - nrm * m_two) + d_y[:, cols]
+            d_mixed[:, cols] = dx.astype(BF16)
+    g_in = dot(corr16[...], d_mixed[...], ((0,), (1,)))
     gain_row = jnp.sum(gain_sum.T, axis=0, keepdims=True)
     at_four = lax.broadcasted_iota(jnp.int32, (16, HID), 0) == 4
     head = jnp.where(at_four, jnp.broadcast_to(gain_row, (16, HID)), head)
     for j in range(3):
         g_in_ref[j * 128 : j * 128 + 128, :] = g_in[:, j * 128 : j * 128 + 128]
     for ref, half in ((keep_ref, core), (send_ref, 1 - core)):
-        for i in range(2):
-            j = half * 2 + i
-            rows = pl.ds(pl.multiple_of(j * HID, HID), HID)
-            part = dot(left[jnp.where(j == 3, 1, 0)], right[rows, :], NT)
-            for n in range(3):
-                at = (i * 3 + n) * HID
-                ref[at : at + HID, :] = part[:, n * 128 : n * 128 + 128].astype(BF16)
         ref[2304:2496, :] = g_in_ref[pl.ds(pl.multiple_of(half * 192, 8), 192), :].astype(BF16)
         part = jnp.where(half == 0, head, 0.0).astype(BF16)
         for n in range(3):
@@ -186,7 +212,7 @@
         ref[2544:HALF, :] = jnp.zeros((HALF - 2544, 128), BF16)
 
 
-def token_grads(pat, ct, w_in_t, gain, w_qkv_t, w_qkv, w_out_t, w_out, w_head):
+def token_grads(pat, ct, w_in, gain, w_qkv_t, w_qkv, w_out_t, w_out, w_head):
     vm = pl.BlockSpec(memory_space=pltpu.VMEM)
     half = jax.ShapeDtypeStruct((HALF, 128), BF16)
     return pl.pallas_call(
@@ -207,9 +233,14 @@
             pltpu.VMEM((8, TOK), F32),
             pltpu.VMEM((HID, 128), F32),
             pltpu.VMEM((HID, 128), F32),
+            pltpu.VMEM((2 * HEADS, 128, 128), F32),
+            pltpu.VMEM((2 * HEADS, 128, 128), BF16),
+            pltpu.VMEM((2 * HEADS, 128, 128), BF16),
+            pltpu.VMEM((2 * HEADS, 128, 128), BF16),
         ],
+        compiler_params=pltpu.CompilerParams(vmem_limit_bytes=28 << 20),
         name="token_grads",
-    )(pat, ct, w_in_t, gain, w_qkv_t, w_qkv, w_out_t, w_out, w_head)
+    )(pat, ct, w_in, gain, w_qkv_t, w_qkv, w_out_t, w_out, w_head)
 
 
 def unpack_kernel(own_ref, other_ref, g_in, g_gain, g_qkv, g_out, g_head):
@@ -253,6 +284,7 @@
         ),
         in_specs=[vm, vm],
         out_specs=(vm,) * 5,
+        compiler_params=pltpu.CompilerParams(vmem_limit_bytes=12 << 20),
         name="unpack",
     )(own, other)
 
@@ -301,7 +333,7 @@
     keep, send = token_grads(
         arrived,
         ct,
-        w_in.T,
+        w_in,
         gain.reshape(1, HID),
         w_qkv.T,
         w_qkv,

time: 118 us -> 104 us (0.88)
  Pallas kernels: 22.4 us -> 12.8 us
  local copies, waits for them, and re-layouts: 9.84 us -> 2.53 us
  waiting for transfers between devices: 14.3 us -> 17.6 us
    pallas_call x1, Pallas kernels: 16.1 us -> 7.81 us  [token_grads(): pl.pallas_call(token_kernel, out_shape=(half, half), in_specs=[vm] * 9, o...]
    unnamed x24 -> x15, local copies, waits for them, and re-layouts: 7.65 us -> 2.1 us
    all_to_all x1, waiting for transfers between devices: 10.6 us -> 14.2 us  [swap(): lax.all_to_all(x, axis, split_axis=0, concat_axis=0, axis_index_groups=gr...]
    pallas_call x1, Pallas kernels: 2.92 us -> 1.64 us  [unpack(): pl.pallas_call(unpack_kernel, out_shape=(jax.ShapeDtypeStruct((128, HID),...]
  transfers between devices with their start and end apart: 3 -> 3, of which waited for: 3 -> 3; matrix products, arithmetic and copies ran while one was open for 4% -> 1% of each run, Pallas kernels for 0% -> 0%
where the time goes in v3:
time: 104 us; the launch traced here: 103 us
  blocking collectives  56.3 us (54%)
  waiting for transfers between devices  17.6 us (17%)
  Pallas kernels  12.8 us (12%)
  starting transfers between devices  12.8 us (12%)
  local copies, waits for them, and re-layouts  2.53 us (2%)
    all_to_all x4, blocking collectives, swap(): lax.all_to_all(x, axis, split_axis=0, concat_axis=0, axis_index_groups=gr...  56.3 us
    all_to_all x1, waiting for transfers between devices, swap(): lax.all_to_all(x, axis, split_axis=0, concat_axis=0, axis_index_groups=gr...  14.2 us
    pallas_call x1, Pallas kernels, token_grads(): pl.pallas_call(token_kernel, out_shape=(half, half), in_specs=[vm] * 9, o...  7.81 us
    all_to_all x1, starting transfers between devices, swap(): lax.all_to_all(x, axis, split_axis=0, concat_axis=0, axis_index_groups=gr...  6.81 us
    ppermute x1, starting transfers between devices, sum_all(): return (x, lax.ppermute(x, 'frame', PARTNER))  4.96 us
    pallas_call x1, Pallas kernels, gather(): pl.pallas_call(gather_kernel, out_shape=jax.ShapeDtypeStruct((8, 544, 128...  3.31 us
    unnamed x15, local copies, waits for them, and re-layouts  2.1 us
  transfers between devices with their start and end apart: 3, of which 3 were waited for; matrix products, arithmetic and copies ran while one was open for 1% of the time, Pallas kernels for 0%

profile of v3, /device:TPU:1, one launch (start us, length us, event | category | flops | bytes accessed | tf_op | source)
XLA Modules:
  0.0 103.2 jit_solution(12778282547154486310)
XLA Ops:
  0.6 3.3 %gather.1 = bf16[8,544,128]{2,1,0:T(8,128)(2,1)} custom-call(s32[1,2,2,16]{3,2,1,0:T(2,128)} %bitcast.17, s32[1,2,16]{2,1,0:T(2,128)} %bitcast.18, s32[1,256]{1,0:T(1,128)} %qf_ref.1, s32[1,256]{1,0:T(1,128)} %qb_ref.1, s32[1,256]{1,0:T(1,128)} %qc_ref.1, bf16[1,2,32,64,128]{4,3,2,1,0:T(8,128)(2,1)} %feats_ref.1), custom_call_target="tpu_custom_call" | custom-call | tf_op jit(solution)/shard_map/gather/pallas_call | solution.py:52
  3.9 0.0 copy-start.5
  3.9 0.0 copy-start.3
  3.9 0.0 copy-start.4
  4.0 0.0 copy-start.1
  4.0 0.0 copy-start
  4.0 6.8 %all-to-all-start = ((bf16[8,544,128]{2,1,0:T(8,128)(2,1)}), bf16[8,544,128]{2,1,0:T(8,128)(2,1)S(1)}, u32[]{:S(2)}, u32[]{:S(2)}) async-start(bf16[8,544,128]{2,1,0:T(8,128)(2,1)} %gather.1), calls=%async_computation | async-start | bytes 2228224 | tf_op jit(solution)/shard_map/all_to_all | solution.py:297
  10.8 0.0 copy-done.5
  10.8 0.0 copy-done.3
  10.8 0.1 copy.20
  10.9 0.1 copy.21
  11.0 0.1 reshape.39
  11.1 0.0 copy-done.4
  11.2 0.0 copy-done.1
  11.2 0.2 copy.23
  11.4 0.0 copy-done
  11.4 0.9 copy.22
  12.3 14.2 %all-to-all-done.pat_ref = bf16[8,544,128]{2,1,0:T(8,128)(2,1)S(1)} async-done(((bf16[8,544,128]{2,1,0:T(8,128)(2,1)}), bf16[8,544,128]{2,1,0:T(8,128)(2,1)S(1)}, u32[]{:S(2)}, u32[]{:S(2)}) %all-to-all-start) | async-done | bytes 1114144 | tf_op jit(solution)/shard_map/all_to_all | solution.py:297
  26.5 0.0 copy-start.2
  26.5 0.9 copy-done.2
  27.4 7.8 %token_grads.1 = (bf16[2560,128]{1,0:T(8,128)(2,1)S(1)}, bf16[2560,128]{1,0:T(8,128)(2,1)S(1)}) custom-call(bf16[8,544,128]{2,1,0:T(8,128)(2,1)S(1)} %all-to-all-done.pat_ref, bf16[16,512]{1,0:T(8,128)(2,1)S(1)} %pad.8.ct_ref, bf16[128,384]{1,0:T(8,128)(2,1)S(1)} %copy-done.2, f32[1,384]{1,0:T(1,128)S(1)} %reshape.40.gain_in, ...), custom_call_target="tpu_custom_call" | custom-call | tf_op jit(solution)/shard_map/token_grads/pallas_call | solution.py:218
  35.2 1.0 %collective-permute-start = (bf16[2560,128]{1,0:T(8,128)(2,1)S(1)}, bf16[2560,128]{1,0:T(8,128)(2,1)S(1)}, u32[]{:S(2)}, u32[]{:S(2)}) collective-permute-start(bf16[2560,128]{1,0:T(8,128)(2,1)S(1)} %get-tuple-element.8), channel_id=1, source_target_pairs={{0,1},{1,0},{2,3},{3,2},{4,5},{5,4},{6,7},{7,6},{8,9},{9,8},{10,11... | collective-permute-start | bytes 1966088 | tf_op jit(solution)/shard_map/ppermute | solution.py:307
  36.2 1.7 %collective-permute-done = bf16[2560,128]{1,0:T(8,128)(2,1)S(1)} collective-permute-done((bf16[2560,128]{1,0:T(8,128)(2,1)S(1)}, bf16[2560,128]{1,0:T(8,128)(2,1)S(1)}, u32[]{:S(2)}, u32[]{:S(2)}) %collective-permute-start) | collective-permute-done | bytes 655392 | tf_op jit(solution)/shard_map/ppermute | solution.py:307
  38.0 0.2 add_convert_fusion
  38.1 13.0 %all_to_all.37 = bf16[4,640,128]{2,1,0:T(8,128)(2,1)S(1)} all-to-all(bf16[4,640,128]{2,1,0:T(8,128)(2,1)S(1)} %bitcast.15), channel_id=1, replica_groups={{0,2,4,6},{1,3,5,7},{8,10,12,14},{9,11,13,15},{16,18,20,22},{17,19,21,2..., dimensions={0} | all-to-all | bytes 1310720 | tf_op jit(solution)/shard_map/all_to_all | solution.py:297
  51.2 0.1 reduce_sum.24
  51.3 19.5 %all_to_all.38 = bf16[32,20,128]{2,1,0:T(8,128)(2,1)S(1)} all-to-all(bf16[32,20,128]{2,1,0:T(8,128)(2,1)S(1)} %all_to_all.27), channel_id=1, replica_groups=mesh['dp'=32,'frame'=8] {'dp'}, dimensions={0} | all-to-all | bytes 327680 | tf_op jit(solution)/shard_map/all_to_all | solution.py:297
  70.9 13.8 %all_to_all.39 = bf16[32,20,128]{2,1,0:T(8,128)(2,1)S(1)} all-to-all(bf16[32,20,128]{2,1,0:T(8,128)(2,1)S(1)} %tile.6), channel_id=1, replica_groups=mesh['dp'=32,'frame'=8] {'dp'}, dimensions={0} | all-to-all | bytes 327680 | tf_op jit(solution)/shard_map/all_to_all | solution.py:297
  84.7 0.1 tile.8
  84.8 10.0 %all_to_all.40 = bf16[4,640,128]{2,1,0:T(8,128)(2,1)S(1)} all-to-all(bf16[4,640,128]{2,1,0:T(8,128)(2,1)S(1)} %tile.8), channel_id=1, replica_groups={{0,2,4,6},{1,3,5,7},{8,10,12,14},{9,11,13,15},{16,18,20,22},{17,19,21,2..., dimensions={0} | all-to-all | bytes 1310720 | tf_op jit(solution)/shard_map/all_to_all | solution.py:297
  94.9 5.0 %collective-permute-start.1 = (bf16[2560,128]{1,0:T(8,128)(2,1)S(1)}, bf16[2560,128]{1,0:T(8,128)(2,1)S(1)}, u32[]{:S(2)}, u32[]{:S(2)}) collective-permute-start(bf16[2560,128]{1,0:T(8,128)(2,1)S(1)} %bitcast.12), channel_id=1, source_target_pairs={{0,1},{1,0},{2,3},{3,2},{4,5},{5,4},{6,7},{7,6},{8,9},{9,8},{10,11... | collective-permute-start | bytes 1966088 | tf_op jit(solution)/shard_map/ppermute | solution.py:312
  99.8 1.7 %collective-permute-done.1.other_ref = bf16[2560,128]{1,0:T(8,128)(2,1)S(1)} collective-permute-done((bf16[2560,128]{1,0:T(8,128)(2,1)S(1)}, bf16[2560,128]{1,0:T(8,128)(2,1)S(1)}, u32[]{:S(2)}, u32[]{:S(2)}) %collective-permute-start.1) | collective-permute-done | bytes 655392 | tf_op jit(solution)/shard_map/ppermute | solution.py:312
  101.6 1.6 %unpack.1 = (f32[128,384]{1,0:T(8,128)}, f32[384]{0:T(512)}, f32[384,1152]{1,0:T(8,128)}, f32[384,384]{1,0:T(8,128)}, f32[4,384]{1,0:T(4,128)}) custom-call(bf16[2560,128]{1,0:T(8,128)(2,1)S(1)} %bitcast.13, bf16[2560,128]{1,0:T(8,128)(2,1)S(1)} %collective-permute-done.1.other_ref), custom_call_target="tpu_custom_call" | custom-call | tf_op jit(solution)/shard_map/unpack/pallas_call | solution.py:276
  (7 shorter events, 0.2 us)
Async XLA Ops:
  3.9 6.8 %copy-start.5 = (f32[384]{0:T(512)S(1)}, f32[384]{0:T(512)}, u32[]{:S(2)}) copy-start(f32[384]{0:T(512)} %param.20) | copy-start | bytes 4612
  3.9 6.8 %copy-start.3 = (bf16[1,4,32,16]{2,3,1,0:T(8,128)(2,1)S(1)}, bf16[1,4,32,16]{2,3,1,0:T(8,128)(2,1)}, u32[]{:S(2)}) copy-start(bf16[1,4,32,16]{2,3,1,0:T(8,128)(2,1)} %param.18) | copy-start | bytes 12292
  3.9 7.2 %copy-start.4 = (bf16[4,384]{1,0:T(4,128)(2,1)S(1)}, bf16[4,384]{1,0:T(4,128)(2,1)}, u32[]{:S(2)}) copy-start(bf16[4,384]{1,0:T(4,128)(2,1)} %param.23) | copy-start | bytes 9220
  4.0 7.2 %copy-start.1 = (bf16[384,384]{1,0:T(8,128)(2,1)S(1)}, bf16[384,384]{1,0:T(8,128)(2,1)}, u32[]{:S(2)}) copy-start(bf16[384,384]{1,0:T(8,128)(2,1)} %w_out.1) | copy-start | bytes 884740
  4.0 7.4 %copy-start = (bf16[384,1152]{1,0:T(8,128)(2,1)S(1)}, bf16[384,1152]{1,0:T(8,128)(2,1)}, u32[]{:S(2)}) copy-start(bf16[384,1152]{1,0:T(8,128)(2,1)} %w_qkv.1) | copy-start | bytes 2654212
  4.0 22.5 %all-to-all-start = ((bf16[8,544,128]{2,1,0:T(8,128)(2,1)}), bf16[8,544,128]{2,1,0:T(8,128)(2,1)S(1)}, u32[]{:S(2)}, u32[]{:S(2)}) async-start(bf16[8,544,128]{2,1,0:T(8,128)(2,1)} %gather.1), calls=%async_computation | async-start | bytes 2228224 | tf_op jit(solution)/shard_map/all_to_all | solution.py:297
  26.5 0.9 copy-start.2
  35.2 2.8 %collective-permute-start = (bf16[2560,128]{1,0:T(8,128)(2,1)S(1)}, bf16[2560,128]{1,0:T(8,128)(2,1)S(1)}, u32[]{:S(2)}, u32[]{:S(2)}) collective-permute-start(bf16[2560,128]{1,0:T(8,128)(2,1)S(1)} %get-tuple-element.8), channel_id=1, source_target_pairs={{0,1},{1,0},{2,3},{3,2},{4,5},{5,4},{6,7},{7,6},{8,9},{9,8},{10,11... | collective-permute-start | bytes 1966088 | tf_op jit(solution)/shard_map/ppermute | solution.py:307
  94.9 6.7 %collective-permute-start.1 = (bf16[2560,128]{1,0:T(8,128)(2,1)S(1)}, bf16[2560,128]{1,0:T(8,128)(2,1)S(1)}, u32[]{:S(2)}, u32[]{:S(2)}) collective-permute-start(bf16[2560,128]{1,0:T(8,128)(2,1)S(1)} %bitcast.12), channel_id=1, source_target_pairs={{0,1},{1,0},{2,3},{3,2},{4,5},{5,4},{6,7},{7,6},{8,9},{9,8},{10,11... | collective-permute-start | bytes 1966088 | tf_op jit(solution)/shard_map/ppermute | solution.py:312

commit v4 on v3

--- a/solution.py
+++ b/solution.py
@@ -1,3 +1,5 @@
+import functools
+
 import jax
 import jax.numpy as jnp
 from jax import lax
@@ -61,13 +63,11 @@
 def token_kernel(
     pat_ref,
     ct_ref,
-    w_in,
+    w_ends,
     gain_in,
     w_qkv_t,
     w_qkv,
-    w_out_t,
     w_out,
-    w_head,
     keep_ref,
     send_ref,
     corr32,
@@ -106,11 +106,11 @@
     gain = gain_ref[...]
     for c in range(2):
         wide = slice(c * 256, c * 256 + 256)
-        dy = dot(w_head[...], ct[:, wide], TN)
+        dy = dot(w_ends[128:144, :], ct[:, wide], TN)
         d_y[:, wide] = dy
         d_y16[:, wide] = dy.astype(BF16)
         d_mixed[:, wide] = dot(w_out[...], d_y16[:, wide]).astype(BF16)
-        x_zero[:, wide] = dot(w_in[...], corr16[wide, :], ((0,), (1,)))
+        x_zero[:, wide] = dot(w_ends[0:128, :], corr16[wide, :], ((0,), (1,)))
         for n in range(2):
             cols = slice(c * 256 + n * 128, c * 256 + n * 128 + 128)
             x0 = x_zero[:, cols]
@@ -185,7 +185,7 @@
     gain_sum = jnp.zeros((HID, 128), F32)
     for c in range(2):
         wide = slice(c * 256, c * 256 + 256)
-        y16 = (x_zero[:, wide] + dot(w_out_t[...], mixed[:, wide])).astype(BF16)
+        y16 = (x_zero[:, wide] + dot(w_out[...], mixed[:, wide], TN)).astype(BF16)
         head = head + dot(ct[:, wide], y16, NT)
         x_zero[:, wide] = dot(w_qkv[...], d_qkv[:, wide])
         for n in range(2):
@@ -212,13 +212,13 @@
         ref[2544:HALF, :] = jnp.zeros((HALF - 2544, 128), BF16)
 
 
-def token_grads(pat, ct, w_in, gain, w_qkv_t, w_qkv, w_out_t, w_out, w_head):
+def token_grads(pat, ct, w_ends, gain, w_qkv_t, w_qkv, w_out):
     vm = pl.BlockSpec(memory_space=pltpu.VMEM)
     half = jax.ShapeDtypeStruct((HALF, 128), BF16)
     return pl.pallas_call(
         token_kernel,
         out_shape=(half, half),
-        in_specs=[vm] * 9,
+        in_specs=[vm] * 7,
         out_specs=(vm, vm),
         scratch_shapes=[
             pltpu.VMEM((TOK, 128), F32),
@@ -240,7 +240,7 @@
         ],
         compiler_params=pltpu.CompilerParams(vmem_limit_bytes=28 << 20),
         name="token_grads",
-    )(pat, ct, w_in, gain, w_qkv_t, w_qkv, w_out_t, w_out, w_head)
+    )(pat, ct, w_ends, gain, w_qkv_t, w_qkv, w_out)
 
 
 def unpack_kernel(own_ref, other_ref, g_in, g_gain, g_qkv, g_out, g_head):
@@ -289,8 +289,17 @@
     )(own, other)
 
 
-Y_GROUPS = [[0, 2, 4, 6], [1, 3, 5, 7]]
+AXES = ("dp", "frame")
 PARTNER = [(i, i ^ 1) for i in range(8)]
+
+
+def make_groups(mesh):
+    nx = max(mesh.shape["dp"] // 8, 1)
+    nz = mesh.shape["dp"] // nx
+    at = lambda x, y, z, c: (x * nz + z) * 8 + y * 2 + c
+    plane = [[at(x, y, z, c) for y in range(4) for x in range(nx)] for z in range(nz) for c in range(2)]
+    line = [[at(x, y, z, c) for z in range(nz)] for x in range(nx) for y in range(4) for c in range(2)]
+    return plane, line
 
 
 def swap(x, axis, groups=None):
@@ -303,16 +312,18 @@
     return jnp.sum(x.reshape(n, x.shape[0] // n, x.shape[1]).astype(F32), axis=0).astype(BF16)
 
 
-def sum_all(keep, send):
+def sum_all(keep, send, groups):
+    plane, line = groups
+    n, m = len(plane[0]), len(line[0])
     x = (keep.astype(F32) + lax.ppermute(send, "frame", PARTNER).astype(F32)).astype(BF16)
-    x = fold(swap(x, "frame", Y_GROUPS), 4)
-    x = fold(swap(x, "dp"), 32)
-    x = swap(jnp.tile(x, (32, 1)), "dp")
-    x = swap(jnp.tile(x, (4, 1)), "frame", Y_GROUPS)
+    x = fold(swap(x, AXES, plane), n)
+    x = fold(swap(jnp.tile(x, (m, 1)), AXES, line), m)
+    x = swap(jnp.tile(x, (n, 1)), AXES, plane)
     return x, lax.ppermute(x, "frame", PARTNER)
 
 
 def body(
+    groups,
     features,
     vis_block,
     vis_count,
@@ -333,15 +344,13 @@
     keep, send = token_grads(
         arrived,
         ct,
-        w_in,
+        jnp.concatenate([w_in, w_head, jnp.zeros((12, HID), BF16)]),
         gain.reshape(1, HID),
         w_qkv.T,
         w_qkv,
-        w_out.T,
         w_out,
-        jnp.pad(w_head, ((0, 12), (0, 0))),
     )
-    return unpack(*sum_all(keep, send))
+    return unpack(*sum_all(keep, send, groups))
 
 
 def solution(mesh):
@@ -360,4 +369,5 @@
         P(),
     )
     out_specs = (P(), P(), P(), P(), P())
-    return jax.shard_map(body, mesh=mesh, in_specs=in_specs, out_specs=out_specs, check_vma=False)
+    step = functools.partial(body, make_groups(mesh))
+    return jax.shard_map(step, mesh=mesh, in_specs=in_specs, out_specs=out_specs, check_vma=False)

time: 104 us -> 93.9 us (0.903)
  blocking collectives: 56.3 us -> 48.8 us
  starting transfers between devices: 12.8 us -> 11.7 us
  local copies, waits for them, and re-layouts: 2.53 us -> 1.44 us
    all_to_all x4 -> x3, blocking collectives: 56.3 us -> 48.8 us  [swap(): lax.all_to_all(x, axis, split_axis=0, concat_axis=0, axis_index_groups=gr...]
    ppermute x1, starting transfers between devices: 4.96 us -> 3.83 us  [sum_all(): return (x, lax.ppermute(x, 'frame', PARTNER))]
    unnamed x15 -> x14, local copies, waits for them, and re-layouts: 2.1 us -> 0.99 us
where the time goes in v4:
time: 93.9 us; the launch traced here: 93.6 us
  blocking collectives  48.8 us (52%)
  waiting for transfers between devices  17.7 us (19%)
  Pallas kernels  12.8 us (14%)
  starting transfers between devices  11.7 us (12%)
  local copies, waits for them, and re-layouts  1.44 us (2%)
    all_to_all x3, blocking collectives, swap(): lax.all_to_all(x, axis, split_axis=0, concat_axis=0, axis_index_groups=gr...  48.8 us
    all_to_all x1, waiting for transfers between devices, swap(): lax.all_to_all(x, axis, split_axis=0, concat_axis=0, axis_index_groups=gr...  14.2 us
    pallas_call x1, Pallas kernels, token_grads(): pl.pallas_call(token_kernel, out_shape=(half, half), in_specs=[vm] * 7, o...  7.84 us
    all_to_all x1, starting transfers between devices, swap(): lax.all_to_all(x, axis, split_axis=0, concat_axis=0, axis_index_groups=gr...  6.81 us
    ppermute x1, starting transfers between devices, sum_all(): return (x, lax.ppermute(x, 'frame', PARTNER))  3.83 us
    pallas_call x1, Pallas kernels, gather(): pl.pallas_call(gather_kernel, out_shape=jax.ShapeDtypeStruct((8, 544, 128...  3.31 us
  transfers between devices with their start and end apart: 3, of which 3 were waited for; matrix products, arithmetic and copies ran while one was open for 1% of the time, Pallas kernels for 0%

profile of v4, /device:TPU:1, one launch (start us, length us, event | category | flops | bytes accessed | tf_op | source)
XLA Modules:
  0.0 93.6 jit_solution(4622391642822844232)
XLA Ops:
  0.6 3.3 %gather.1 = bf16[8,544,128]{2,1,0:T(8,128)(2,1)} custom-call(s32[1,2,2,16]{3,2,1,0:T(2,128)} %bitcast.15, s32[1,2,16]{2,1,0:T(2,128)} %bitcast.16, s32[1,256]{1,0:T(1,128)} %qf_ref.1, s32[1,256]{1,0:T(1,128)} %qb_ref.1, s32[1,256]{1,0:T(1,128)} %qc_ref.1, bf16[1,2,32,64,128]{4,3,2,1,0:T(8,128)(2,1)} %feats_ref.1), custom_call_target="tpu_custom_call" | custom-call | tf_op jit(solution)/shard_map/gather/pallas_call | solution.py:54
  3.9 0.0 copy-start.5
  3.9 0.0 copy-start.3
  3.9 0.0 copy-start
  4.0 6.8 %all-to-all-start = ((bf16[8,544,128]{2,1,0:T(8,128)(2,1)}), bf16[8,544,128]{2,1,0:T(8,128)(2,1)S(1)}, u32[]{:S(2)}, u32[]{:S(2)}) async-start(bf16[8,544,128]{2,1,0:T(8,128)(2,1)} %gather.1), calls=%async_computation | async-start | bytes 2228224 | tf_op jit(solution)/shard_map/all_to_all | solution.py:306
  10.8 0.0 copy-done.5
  10.8 0.0 copy-start.2
  10.8 0.0 copy-start.4
  10.8 0.0 copy-start.1
  10.8 0.0 copy-done.3
  10.8 0.1 copy.22
  10.9 0.1 copy.23
  11.0 0.1 reshape.36
  11.1 0.0 copy-done
  11.2 0.9 copy.24
  12.1 0.1 pad.7.clone
  12.1 0.0 copy-done.2
  12.1 0.0 copy-done.4
  12.1 0.1 maximum_maximum_fusion.w_ends
  12.2 14.2 %all-to-all-done.pat_ref = bf16[8,544,128]{2,1,0:T(8,128)(2,1)S(1)} async-done(((bf16[8,544,128]{2,1,0:T(8,128)(2,1)}), bf16[8,544,128]{2,1,0:T(8,128)(2,1)S(1)}, u32[]{:S(2)}, u32[]{:S(2)}) %all-to-all-start) | async-done | bytes 1114144 | tf_op jit(solution)/shard_map/all_to_all | solution.py:306
  26.5 0.0 copy-done.1
  26.5 7.8 %token_grads.1 = (bf16[2560,128]{1,0:T(8,128)(2,1)S(1)}, bf16[2560,128]{1,0:T(8,128)(2,1)S(1)}) custom-call(bf16[8,544,128]{2,1,0:T(8,128)(2,1)S(1)} %all-to-all-done.pat_ref, bf16[16,512]{1,0:T(8,128)(2,1)S(1)} %pad.4.ct_ref, bf16[144,384]{1,0:T(8,128)(2,1)S(1)} %maximum_maximum_fusion.w_ends, f32[1,384]{1,0:T(1,128)S(1)} %reshape.37.gain_in, ...), custom_call_target="tpu_custom_call" | custom-call | tf_op jit(solution)/shard_map/token_grads/pallas_call | solution.py:218
  34.3 1.1 %collective-permute-start = (bf16[2560,128]{1,0:T(8,128)(2,1)S(1)}, bf16[2560,128]{1,0:T(8,128)(2,1)S(1)}, u32[]{:S(2)}, u32[]{:S(2)}) collective-permute-start(bf16[2560,128]{1,0:T(8,128)(2,1)S(1)} %get-tuple-element.8), channel_id=1, source_target_pairs={{0,1},{1,0},{2,3},{3,2},{4,5},{5,4},{6,7},{7,6},{8,9},{9,8},{10,11... | collective-permute-start | bytes 1966088 | tf_op jit(solution)/shard_map/ppermute | solution.py:318
  35.4 1.7 %collective-permute-done = bf16[2560,128]{1,0:T(8,128)(2,1)S(1)} collective-permute-done((bf16[2560,128]{1,0:T(8,128)(2,1)S(1)}, bf16[2560,128]{1,0:T(8,128)(2,1)S(1)}, u32[]{:S(2)}, u32[]{:S(2)}) %collective-permute-start) | collective-permute-done | bytes 655392 | tf_op jit(solution)/shard_map/ppermute | solution.py:318
  37.1 0.2 add_convert_fusion
  37.3 16.2 %all_to_all.28 = bf16[16,160,128]{2,1,0:T(8,128)(2,1)S(1)} all-to-all(bf16[16,160,128]{2,1,0:T(8,128)(2,1)S(1)} %bitcast.13), channel_id=1, replica_groups={{0,64,128,192,2,66,130,194,4,68,132,196,6,70,134,198},{1,65,129,193,3,6..., dimensions={0} | all-to-all | bytes 1310720 | tf_op jit(solution)/shard_map/all_to_all | solution.py:306
  53.5 0.1 reduce_sum.24
  53.6 18.8 %all_to_all.29 = bf16[8,160,128]{2,1,0:T(8,128)(2,1)S(1)} all-to-all(bf16[8,160,128]{2,1,0:T(8,128)(2,1)S(1)} %tile.4), channel_id=1, replica_groups={{0,8,16,24,32,40,48,56},{1,9,17,25,33,41,49,57},{2,10,18,26,34,42,50,58..., dimensions={0} | all-to-all | bytes 655360 | tf_op jit(solution)/shard_map/all_to_all | solution.py:306
  72.5 0.1 tile.5
  72.5 13.9 %all_to_all.30 = bf16[16,160,128]{2,1,0:T(8,128)(2,1)S(1)} all-to-all(bf16[16,160,128]{2,1,0:T(8,128)(2,1)S(1)} %tile.5), channel_id=1, replica_groups={{0,64,128,192,2,66,130,194,4,68,132,196,6,70,134,198},{1,65,129,193,3,6..., dimensions={0} | all-to-all | bytes 1310720 | tf_op jit(solution)/shard_map/all_to_all | solution.py:306
  86.4 3.8 %collective-permute-start.1 = (bf16[2560,128]{1,0:T(8,128)(2,1)S(1)}, bf16[2560,128]{1,0:T(8,128)(2,1)S(1)}, u32[]{:S(2)}, u32[]{:S(2)}) collective-permute-start(bf16[2560,128]{1,0:T(8,128)(2,1)S(1)} %bitcast.11), channel_id=1, source_target_pairs={{0,1},{1,0},{2,3},{3,2},{4,5},{5,4},{6,7},{7,6},{8,9},{9,8},{10,11... | collective-permute-start | bytes 1966088 | tf_op jit(solution)/shard_map/ppermute | solution.py:322
  90.3 1.7 %collective-permute-done.1.other_ref = bf16[2560,128]{1,0:T(8,128)(2,1)S(1)} collective-permute-done((bf16[2560,128]{1,0:T(8,128)(2,1)S(1)}, bf16[2560,128]{1,0:T(8,128)(2,1)S(1)}, u32[]{:S(2)}, u32[]{:S(2)}) %collective-permute-start.1) | collective-permute-done | bytes 655392 | tf_op jit(solution)/shard_map/ppermute | solution.py:322
  92.0 1.6 %unpack.1 = (f32[128,384]{1,0:T(8,128)}, f32[384]{0:T(512)}, f32[384,1152]{1,0:T(8,128)}, f32[384,384]{1,0:T(8,128)}, f32[4,384]{1,0:T(4,128)}) custom-call(bf16[2560,128]{1,0:T(8,128)(2,1)S(1)} %bitcast.12, bf16[2560,128]{1,0:T(8,128)(2,1)S(1)} %collective-permute-done.1.other_ref), custom_call_target="tpu_custom_call" | custom-call | tf_op jit(solution)/shard_map/unpack/pallas_call | solution.py:276
  (5 shorter events, 0.1 us)
Async XLA Ops:
  3.9 6.8 %copy-start.5 = (f32[384]{0:T(512)S(1)}, f32[384]{0:T(512)}, u32[]{:S(2)}) copy-start(f32[384]{0:T(512)} %param.20) | copy-start | bytes 4612
  3.9 6.9 %copy-start.3 = (bf16[1,4,32,16]{2,3,1,0:T(8,128)(2,1)S(1)}, bf16[1,4,32,16]{2,3,1,0:T(8,128)(2,1)}, u32[]{:S(2)}) copy-start(bf16[1,4,32,16]{2,3,1,0:T(8,128)(2,1)} %param.18) | copy-start | bytes 12292
  3.9 7.2 %copy-start = (bf16[384,1152]{1,0:T(8,128)(2,1)S(1)}, bf16[384,1152]{1,0:T(8,128)(2,1)}, u32[]{:S(2)}) copy-start(bf16[384,1152]{1,0:T(8,128)(2,1)} %w_qkv.1) | copy-start | bytes 2654212
  4.0 22.5 %all-to-all-start = ((bf16[8,544,128]{2,1,0:T(8,128)(2,1)}), bf16[8,544,128]{2,1,0:T(8,128)(2,1)S(1)}, u32[]{:S(2)}, u32[]{:S(2)}) async-start(bf16[8,544,128]{2,1,0:T(8,128)(2,1)} %gather.1), calls=%async_computation | async-start | bytes 2228224 | tf_op jit(solution)/shard_map/all_to_all | solution.py:306
  10.8 1.4 %copy-start.2 = (bf16[128,384]{1,0:T(8,128)(2,1)S(1)}, bf16[128,384]{1,0:T(8,128)(2,1)}, u32[]{:S(2)}) copy-start(bf16[128,384]{1,0:T(8,128)(2,1)} %param.19) | copy-start | bytes 294916
  10.8 1.4 %copy-start.4 = (bf16[4,384]{1,0:T(4,128)(2,1)S(1)}, bf16[4,384]{1,0:T(4,128)(2,1)}, u32[]{:S(2)}) copy-start(bf16[4,384]{1,0:T(4,128)(2,1)} %param.23) | copy-start | bytes 9220
  10.8 15.7 %copy-start.1 = (bf16[384,384]{1,0:T(8,128)(2,1)S(1)}, bf16[384,384]{1,0:T(8,128)(2,1)}, u32[]{:S(2)}) copy-start(bf16[384,384]{1,0:T(8,128)(2,1)} %w_out.1) | copy-start | bytes 884740
  34.3 2.8 %collective-permute-start = (bf16[2560,128]{1,0:T(8,128)(2,1)S(1)}, bf16[2560,128]{1,0:T(8,128)(2,1)S(1)}, u32[]{:S(2)}, u32[]{:S(2)}) collective-permute-start(bf16[2560,128]{1,0:T(8,128)(2,1)S(1)} %get-tuple-element.8), channel_id=1, source_target_pairs={{0,1},{1,0},{2,3},{3,2},{4,5},{5,4},{6,7},{7,6},{8,9},{9,8},{10,11... | collective-permute-start | bytes 1966088 | tf_op jit(solution)/shard_map/ppermute | solution.py:318
  86.4 5.6 %collective-permute-start.1 = (bf16[2560,128]{1,0:T(8,128)(2,1)S(1)}, bf16[2560,128]{1,0:T(8,128)(2,1)S(1)}, u32[]{:S(2)}, u32[]{:S(2)}) collective-permute-start(bf16[2560,128]{1,0:T(8,128)(2,1)S(1)} %bitcast.11), channel_id=1, source_target_pairs={{0,1},{1,0},{2,3},{3,2},{4,5},{5,4},{6,7},{7,6},{8,9},{9,8},{10,11... | collective-permute-start | bytes 1966088 | tf_op jit(solution)/shard_map/ppermute | solution.py:322
